TPU v7x, 256 devices: a whole 4x4x8 slice. The times are simulated.
256 devices in a mesh: dom: 32 (over y, x, core), band: 8 (over z).
Axes of the slice: x: 4, y: 4, z: 8, core: 2. Of those that a mesh axis runs over, the one named last changes fastest.
Arguments:
- orbitals: bfloat16 [768, 32, 6, 1152], P('band', 'dom'), may hold values from -6 to 6
- occupations: float32 [768], P('band'), may hold values from 0.2 to 2
- previous: float32 [32, 12, 4608], P('dom'), may hold values from -6 to 6
- compensation: float32 [32, 12, 4608], P('dom'), may hold values from 0 to 1.5
- local_potential: float32 [32, 6, 1152], P('dom'), may hold values from -6 to 6
Outputs:
- applied: bfloat16 [768, 32, 6, 1152], P('band', 'dom')
- potential: float32 [32, 12, 4608], P('dom')
All inputs are finite; a program needn't handle non-finite values.
Results may differ from a plain program's by a relative error of at most 0.001.
Values may be sent and summed in bfloat16 or wider, within the bound.
A program may use at most 64 MiB of HBM per device.

v0:
```python
import math

import jax
import jax.numpy as jnp
from jax import lax
from jax.sharding import PartitionSpec as P

BANDS = 768
BX = 6
BY = 24
BZ = 48
SWEEPS = 4


precise = lax.Precision.HIGHEST


def passed_along(block, axis, distance):
    devices = range(lax.axis_size(axis))
    route = [(i - distance, i) for i in devices if i - distance in devices]
    return lax.ppermute(block, axis, route)


def sent_to_all(x, axis):
    devices = lax.axis_size(axis)
    return lax.all_to_all(jnp.broadcast_to(x[None], (devices, *x.shape)), axis, 0, 0, tiled=True)


def taken_together(x, axis):
    return sent_to_all(x, axis).sum(axis=0)


def neighbour(extended):
    total = extended[..., 2:, 1:-1, 1:-1] + extended[..., :-2, 1:-1, 1:-1]
    total = total + extended[..., 1:-1, 2:, 1:-1] + extended[..., 1:-1, :-2, 1:-1]
    return total + extended[..., 1:-1, 1:-1, 2:] + extended[..., 1:-1, 1:-1, :-2]


def refine_axis(padded, along):
    front = jnp.moveaxis(padded, along, 0)
    middle = front[1:-1]
    even_rows = 0.75 * middle + 0.25 * front[:-2]
    odd_rows = 0.75 * middle + 0.25 * front[2:]
    refined = jnp.stack([even_rows, odd_rows], 1).reshape((2 * middle.shape[0],) + middle.shape[1:])
    return jnp.moveaxis(refined, 0, along)


def coarsen_axis(padded, along):
    front = jnp.moveaxis(padded, along, 0)
    half_rows = (front.shape[0] - 2) // 2
    middle = front[1:-1].reshape((half_rows, 2) + front.shape[1:])
    left_rows = front[0 : 2 * half_rows : 2]
    right_rows = front[3 : 2 * half_rows + 2 : 2]
    coarse = 0.5 * (
        0.25 * left_rows + 0.75 * middle[:, 0] + 0.75 * middle[:, 1] + 0.25 * right_rows
    )
    return jnp.moveaxis(coarse, 0, along)


def extend(array_in, width, layout, sender):
    coords, counts, strides = layout
    for axis_pos in range(3):
        along = array_in.ndim - 3 + axis_pos
        length = array_in.shape[along]
        upper_rim = lax.slice_in_dim(array_in, length - width, length, axis=along)
        lower_rim = lax.slice_in_dim(array_in, 0, width, axis=along)
        from_below = sender(upper_rim, strides[axis_pos])
        from_above = sender(lower_rim, -strides[axis_pos])
        from_below = jnp.where(coords[axis_pos] > 0, from_below, jnp.zeros_like(from_below))
        from_above = jnp.where(
            coords[axis_pos] < counts[axis_pos] - 1, from_above, jnp.zeros_like(from_above)
        )
        array_in = jnp.concatenate([from_below, array_in, from_above], along)
    return array_in


def send_orbital(rim_piece, offset):
    return passed_along(rim_piece, "dom", offset)


def send_density(rim_piece, offset):
    return passed_along(rim_piece, "dom", offset)


def send_deep(rim_piece, offset):
    return passed_along(rim_piece.astype(jnp.bfloat16), "dom", offset).astype(rim_piece.dtype)


def local(orbitals, occupations, previous, compensation, local_potential):
    domains = lax.axis_size("dom")
    split_z = 2
    split_y = min(4, domains // 4)
    split_x = domains // (split_y * split_z)
    position = lax.axis_index("dom")
    coords = (position // (split_y * split_z), position // split_z % split_y, position % split_z)
    counts = (split_x, split_y, split_z)
    strides = (split_y * split_z, split_z, 1)
    layout = (coords, counts, strides)
    local_bands = orbitals.shape[0]
    orbital_cube = orbitals.reshape(local_bands, BX, BY, BZ)
    wave_field = orbital_cube.astype(jnp.float32)
    extended = extend(orbital_cube, 1, layout, send_orbital).astype(jnp.float32)
    laplace = neighbour(extended) - 6.0 * wave_field
    squares = (wave_field * wave_field).reshape(local_bands, BX * BY * BZ)
    partial_value = jnp.dot(occupations, squares, precision=precise).reshape(BX, BY, BZ)
    density = taken_together(partial_value, "band") / BANDS
    refined = refine_axis(extend(density, 1, layout, send_density), 0)
    refined = refine_axis(refined, 1)
    refined = refine_axis(refined, 2)
    source = math.pi * (refined - compensation.reshape(2 * BX, 2 * BY, 2 * BZ))
    start_field = previous.reshape(2 * BX, 2 * BY, 2 * BZ)
    margin = SWEEPS + 1
    stacked = extend(jnp.stack([start_field, source]), margin, layout, send_deep)
    extended = stacked[0]
    wide_source = stacked[1][1:-1, 1:-1, 1:-1]
    boxes = (2 * BX, 2 * BY, 2 * BZ)
    valid_axes = []
    for axis_pos in range(3):
        places = (
            coords[axis_pos] * boxes[axis_pos] + jnp.arange(boxes[axis_pos] + 2 * margin) - margin
        )
        within = (places >= 0) & (places < boxes[axis_pos] * counts[axis_pos])
        valid_axes.append(within[1:-1])
    inside = (
        valid_axes[0][:, None, None] & valid_axes[1][None, :, None] & valid_axes[2][None, None, :]
    )
    for counter in range(SWEEPS):
        updated = jnp.where(inside, (neighbour(extended) + wide_source) / 6.0, 0.0)
        extended = extended.at[1:-1, 1:-1, 1:-1].set(updated)
    potential = extended[margin:-margin, margin:-margin, margin:-margin]
    potential_rim = extended[
        margin - 1 : 1 - margin, margin - 1 : 1 - margin, margin - 1 : 1 - margin
    ]
    coarse = coarsen_axis(potential_rim, 0)
    coarse = coarsen_axis(coarse, 1)
    coarse = coarsen_axis(coarse, 2)
    effective = coarse - jnp.cbrt(3.0 / math.pi * density) + local_potential.reshape(BX, BY, BZ)
    applied = (-0.5 * laplace + effective[None] * wave_field).astype(jnp.bfloat16)
    return (applied.reshape(orbitals.shape), potential.reshape(previous.shape))


def solution(mesh):
    return jax.shard_map(
        local,
        mesh=mesh,
        in_specs=(
            P("band", "dom", None, None),
            P("band"),
            P("dom", None, None),
            P("dom", None, None),
            P("dom", None, None),
        ),
        out_specs=(P("band", "dom", None, None), P("dom", None, None)),
        check_vma=False,
    )
```

profile of v0, /device:TPU:1, one launch (start us, length us, event | category | flops | bytes accessed | tf_op | source)
XLA Modules:
  0.0 191.6 jit_solution(10612514883214091951)
XLA Ops:
  3.6 4.7 %collective-permute-start = (bf16[96,1,24,48]{0,3,2,1:T(8,128)(2,1)}, bf16[96,1,24,48]{0,3,2,1:T(8,128)(2,1)}, u32[]{:S(2)}, u32[]{:S(2)}) collective-permute-start(bf16[96,1,24,48]{0,3,2,1:T(8,128)(2,1)} %get-tuple-element.62), channel_id=1, source_target_pairs={{0,64},{8,72},{16,80},{24,88},{32,96},{40,104},{48,112},{56,120},{... | collective-permute-start | bytes 663560 | tf_op jit(solution)/shard_map/ppermute | solution.py:21
  11.5 3.6 %copy.66 = f32[6912,96]{1,0:T(8,128)} copy(f32[6912,96]{0,1:T(8,128)} %bitcast.133) | data formatting | bytes 5308416 | tf_op jit(solution)/shard_map/dot_general | solution.py:105
  15.2 12.2 %fusion.43 = f32[1,6,24,48]{3,0,2,1:T(1,128)S(1)} fusion(f32[6,24,48,96]{3,2,1,0:T(8,128)} %bitcast.132, f32[96]{0:T(128)S(1)} %copy-done), kind=kOutput, calls=%fused_computation.142 | convolution fusion | flops 7962624 | bytes 2682240 | tf_op jit(solution)/shard_map/dot_general | solution.py:105
  28.7 8.2 %all-to-all-start = ((f32[8,1,6912]{2,1,0:T(1,128)}), f32[8,1,6912]{2,1,0:T(1,128)S(1)}, u32[]{:S(2)}, u32[]{:S(2)}) async-start(f32[8,1,6912]{2,1,0:T(1,128)} %reshape.237), calls=%async_computation | async-start | bytes 442368 | tf_op jit(solution)/shard_map/all_to_all | solution.py:26
  40.8 3.7 %collective-permute-start.2 = (bf16[96,8,1,48]{0,3,2,1:T(8,128)(2,1)}, bf16[96,8,1,48]{0,3,2,1:T(8,128)(2,1)}, u32[]{:S(2)}, u32[]{:S(2)}) collective-permute-start(bf16[96,8,1,48]{0,3,2,1:T(8,128)(2,1)} %get-tuple-element.60), channel_id=1, source_target_pairs={{0,16},{8,24},{16,32},{24,40},{32,48},{40,56},{48,64},{56,72},{64,... | collective-permute-start | bytes 221192 | tf_op jit(solution)/shard_map/ppermute | solution.py:21
  48.4 7.0 %collective-permute-start.6 = (f32[1,24,48]{2,1,0:T(8,128)S(1)}, f32[1,24,48]{2,1,0:T(8,128)S(1)}, u32[]{:S(2)}, u32[]{:S(2)}) collective-permute-start(f32[1,24,48]{2,1,0:T(8,128)S(1)} %get-tuple-element.86), channel_id=1, source_target_pairs={{0,64},{8,72},{16,80},{24,88},{32,96},{40,104},{48,112},{56,120},{... | collective-permute-start | bytes 13832 | tf_op jit(solution)/shard_map/ppermute | solution.py:21
  56.7 3.1 %collective-permute-done.7 = f32[1,24,48]{2,1,0:T(8,128)S(1)} collective-permute-done((f32[1,24,48]{2,1,0:T(8,128)S(1)}, f32[1,24,48]{2,1,0:T(8,128)S(1)}, u32[]{:S(2)}, u32[]{:S(2)}) %collective-permute-start.7) | collective-permute-done | bytes 4640 | tf_op jit(solution)/shard_map/ppermute | solution.py:21
  64.0 3.0 %collective-permute-done.9 = f32[8,1,48]{2,1,0:T(1,128)S(1)} collective-permute-done((f32[8,1,48]{2,1,0:T(1,128)S(1)}, f32[8,1,48]{2,1,0:T(1,128)S(1)}, u32[]{:S(2)}, u32[]{:S(2)}) %collective-permute-start.9) | collective-permute-done | bytes 1568 | tf_op jit(solution)/shard_map/ppermute | solution.py:21
  67.2 7.9 %collective-permute-start.10 = (f32[8,26,1]{2,1,0:T(8,128)S(1)}, f32[8,26,1]{2,1,0:T(8,128)S(1)}, u32[]{:S(2)}, u32[]{:S(2)}) collective-permute-start(f32[8,26,1]{2,1,0:T(8,128)S(1)} %get-tuple-element.82), channel_id=1, source_target_pairs={{0,8},{8,16},{16,24},{24,32},{32,40},{40,48},{48,56},{56,64},{64,7... | collective-permute-start | bytes 2504 | tf_op jit(solution)/shard_map/ppermute | solution.py:21
  78.0 3.0 %collective-permute-start.5 = (bf16[96,8,26,1]{0,3,2,1:T(2,128)(2,1)}, bf16[96,8,26,1]{0,3,2,1:T(2,128)(2,1)}, u32[]{:S(2)}, u32[]{:S(2)}) collective-permute-start(bf16[96,8,26,1]{0,3,2,1:T(2,128)(2,1)} %get-tuple-element.59), channel_id=1, source_target_pairs={{8,0},{16,8},{24,16},{32,24},{40,32},{48,40},{56,48},{64,56},{72,6... | collective-permute-start | bytes 119816 | tf_op jit(solution)/shard_map/ppermute | solution.py:21
  81.0 2.1 %collective-permute-start.11 = (f32[8,26,1]{2,1,0:T(8,128)S(1)}, f32[8,26,1]{2,1,0:T(8,128)S(1)}, u32[]{:S(2)}, u32[]{:S(2)}) collective-permute-start(f32[8,26,1]{2,1,0:T(8,128)S(1)} %get-tuple-element.83), channel_id=1, source_target_pairs={{8,0},{16,8},{24,16},{32,24},{40,32},{48,40},{56,48},{64,56},{72,6... | collective-permute-start | bytes 2504 | tf_op jit(solution)/shard_map/ppermute | solution.py:21
  83.1 4.1 %collective-permute-done.11 = f32[8,26,1]{2,1,0:T(8,128)S(1)} collective-permute-done((f32[8,26,1]{2,1,0:T(8,128)S(1)}, f32[8,26,1]{2,1,0:T(8,128)S(1)}, u32[]{:S(2)}, u32[]{:S(2)}) %collective-permute-start.11) | collective-permute-done | bytes 864 | tf_op jit(solution)/shard_map/ppermute | solution.py:21
  96.4 4.3 %collective-permute-done.13 = bf16[2,5,48,96]{3,2,1,0:T(8,128)(2,1)S(1)} collective-permute-done((bf16[2,5,48,96]{3,2,1,0:T(8,128)(2,1)S(1)}, bf16[2,5,48,96]{3,2,1,0:T(8,128)(2,1)S(1)}, u32[]{:S(2)}, u32[]{:S(2)}) %collective-permute-start.13) | collective-permute-done | bytes 92192 | tf_op jit(solution)/shard_map/ppermute | solution.py:21
  100.8 4.4 %collective-permute-start.14 = (bf16[2,22,5,96]{3,2,1,0:T(8,128)(2,1)S(1)}, bf16[2,22,5,96]{3,2,1,0:T(8,128)(2,1)S(1)}, u32[]{:S(2)}, u32[]{:S(2)}) collective-permute-start(bf16[2,22,5,96]{3,2,1,0:T(8,128)(2,1)S(1)} %get-tuple-element.66), channel_id=1, source_target_pairs={{0,16},{8,24},{16,32},{24,40},{32,48},{40,56},{48,64},{56,72},{64,... | collective-permute-start | bytes 126728 | tf_op jit(solution)/shard_map/ppermute | solution.py:21
  107.3 5.4 %collective-permute-done.15 = bf16[2,22,5,96]{3,2,1,0:T(8,128)(2,1)S(1)} collective-permute-done((bf16[2,22,5,96]{3,2,1,0:T(8,128)(2,1)S(1)}, bf16[2,22,5,96]{3,2,1,0:T(8,128)(2,1)S(1)}, u32[]{:S(2)}, u32[]{:S(2)}) %collective-permute-start.15) | collective-permute-done | bytes 42272 | tf_op jit(solution)/shard_map/ppermute | solution.py:21
  114.4 2.1 %copy.73 = bf16[2,22,58,5]{2,0,3,1:T(2,128)(2,1)} copy(bf16[2,22,58,5]{3,2,1,0:T(8,128)(2,1)} %get-tuple-element.68) | data formatting | bytes 51040 | tf_op jit(solution)/shard_map/slice | solution.py:65
  116.5 4.1 %collective-permute-start.16 = (bf16[2,22,58,5]{2,0,3,1:T(2,128)(2,1)}, bf16[2,22,58,5]{2,0,3,1:T(2,128)(2,1)}, u32[]{:S(2)}, u32[]{:S(2)}) collective-permute-start(bf16[2,22,58,5]{2,0,3,1:T(2,128)(2,1)} %copy.73), channel_id=1, source_target_pairs={{0,8},{8,16},{16,24},{24,32},{32,40},{40,48},{48,56},{56,64},{64,7... | collective-permute-start | bytes 76568 | tf_op jit(solution)/shard_map/ppermute | solution.py:21
  120.6 6.0 %maximum_convert_fusion = f32[96,8,26,50]{0,3,2,1:T(8,128)} fusion(bf16[96,8,26,1]{0,3,2,1:T(2,128)(2,1)} %broadcast_select_fusion.4, bf16[96,8,1,48]{0,3,2,1:T(8,128)(2,1)} %copy-done.9, bf16[96,1,24,48]{0,3,2,1:T(8,128)(2,1)S(1)} %broadcast_select_fusion.2, bf16[96,6,24,48]{0,3,2,1:T(8,128)(2,1)S(1)} %bitcast.130, ...), kind=kLoop, calls=%fused_computation.11 | loop fusion | flops 13977600 | bytes 5990400 | tf_op jit(solution)/shard_map/convert_element_type | solution.py:102
  130.1 2.3 %copy.74 = f32[2,22,58,5]{3,2,1,0:T(8,128)} copy(bf16[2,22,58,5]{2,0,3,1:T(2,128)(2,1)} %collective-permute-done.16) | data formatting | bytes 76560 | tf_op jit(solution)/shard_map/convert_element_type | solution.py:86
  132.4 2.6 %broadcast_select_fusion.1 = f32[2,22,58,5]{3,2,1,0:T(8,128)} fusion(f32[2,22,58,5]{3,2,1,0:T(8,128)} %copy.74, pred[]{:T(512)S(6)} %gt.6), kind=kLoop, calls=%fused_computation.22 | loop fusion | flops 12760 | bytes 102081 | tf_op jit(solution)/shard_map/jit(_where)/select_n | solution.py:69
  140.9 9.8 %scatter.10 = f32[22,58,106]{2,1,0:T(8,128)S(1)} dynamic-update-slice(f32[22,58,106]{2,1,0:T(8,128)S(1)} %get-tuple-element.65, f32[20,56,104]{2,1,0:T(8,128)} %and_select_fusion.3, s32[]{:T(128)} %constant.182.clone.1, s32[]{:T(128)} %constant.182.clone.1, s32[]{:T(128)} %constant.182.clone.1) | dynamic-update-slice | bytes 931844 | tf_op jit(solution)/shard_map/scatter | solution.py:129
  152.6 9.8 %scatter.11 = f32[22,58,106]{2,1,0:T(8,128)S(1)} dynamic-update-slice(f32[22,58,106]{2,1,0:T(8,128)S(1)} %scatter.10, f32[20,56,104]{2,1,0:T(8,128)} %and_select_fusion.2, s32[]{:T(128)} %constant.182.clone.1, s32[]{:T(128)} %constant.182.clone.1, s32[]{:T(128)} %constant.182.clone.1) | dynamic-update-slice | bytes 931844 | tf_op jit(solution)/shard_map/scatter | solution.py:129
  164.3 9.8 %scatter.14 = f32[22,58,106]{2,1,0:T(8,128)S(1)} dynamic-update-slice(f32[22,58,106]{2,1,0:T(8,128)S(1)} %scatter.11, f32[20,56,104]{2,1,0:T(8,128)} %and_select_fusion.1, s32[]{:T(128)} %constant.182.clone.1, s32[]{:T(128)} %constant.182.clone.1, s32[]{:T(128)} %constant.182.clone.1) | dynamic-update-slice | bytes 931844 | tf_op jit(solution)/shard_map/scatter | solution.py:129
  179.8 10.2 %fusion.3 = bf16[96,6,24,48]{0,3,2,1:T(8,128)(2,1)S(1)} fusion(bf16[96,6,24,48]{0,3,2,1:T(8,128)(2,1)S(1)} %bitcast.131, f32[96,8,26,50]{0,3,2,1:T(8,128)} %maximum_convert_fusion, f32[6,24,48]{2,1,0:T(8,128)S(1)} %fusion.37), kind=kLoop, calls=%fused_computation.5 | loop fusion | flops 7962624 | bytes 18607104 | tf_op jit(solution)/shard_map/convert_element_type | solution.py:138
  (146 shorter events, 56.6 us)
Async XLA Ops:
  3.6 36.4 %collective-permute-start = (bf16[96,1,24,48]{0,3,2,1:T(8,128)(2,1)}, bf16[96,1,24,48]{0,3,2,1:T(8,128)(2,1)}, u32[]{:S(2)}, u32[]{:S(2)}) collective-permute-start(bf16[96,1,24,48]{0,3,2,1:T(8,128)(2,1)} %get-tuple-element.62), channel_id=1, source_target_pairs={{0,64},{8,72},{16,80},{24,88},{32,96},{40,104},{48,112},{56,120},{... | collective-permute-start | bytes 663560 | tf_op jit(solution)/shard_map/ppermute | solution.py:21
  8.4 31.7 %collective-permute-start.1 = (bf16[96,1,24,48]{0,3,2,1:T(8,128)(2,1)}, bf16[96,1,24,48]{0,3,2,1:T(8,128)(2,1)S(1)}, u32[]{:S(2)}, u32[]{:S(2)}) collective-permute-start(bf16[96,1,24,48]{0,3,2,1:T(8,128)(2,1)} %get-tuple-element.63), channel_id=1, source_target_pairs={{64,0},{72,8},{80,16},{88,24},{96,32},{104,40},{112,48},{120,56},{... | collective-permute-start | bytes 663560 | tf_op jit(solution)/shard_map/ppermute | solution.py:21
  15.2 21.9 %copy-start.15 = (f32[1,6,1152]{2,0,1:T(1,128)S(1)}, f32[1,6,1152]{2,0,1:T(1,128)}, u32[]{:S(2)}) copy-start(f32[1,6,1152]{2,0,1:T(1,128)} %param.17) | copy-start | bytes 82948
  15.2 22.7 %copy-start.13 = (f32[1,12,4608]{2,0,1:T(1,128)S(1)}, f32[1,12,4608]{2,0,1:T(1,128)}, u32[]{:S(2)}) copy-start(f32[1,12,4608]{2,0,1:T(1,128)} %param.15) | copy-start | bytes 663556
  15.2 23.4 %copy-start.14 = (f32[1,12,4608]{2,0,1:T(1,128)S(1)}, f32[1,12,4608]{2,0,1:T(1,128)}, u32[]{:S(2)}) copy-start(f32[1,12,4608]{2,0,1:T(1,128)} %param.16) | copy-start | bytes 663556
  28.7 17.6 %all-to-all-start = ((f32[8,1,6912]{2,1,0:T(1,128)}), f32[8,1,6912]{2,1,0:T(1,128)S(1)}, u32[]{:S(2)}, u32[]{:S(2)}) async-start(f32[8,1,6912]{2,1,0:T(1,128)} %reshape.237), calls=%async_computation | async-start | bytes 442368 | tf_op jit(solution)/shard_map/all_to_all | solution.py:26
  40.8 14.5 %collective-permute-start.2 = (bf16[96,8,1,48]{0,3,2,1:T(8,128)(2,1)}, bf16[96,8,1,48]{0,3,2,1:T(8,128)(2,1)}, u32[]{:S(2)}, u32[]{:S(2)}) collective-permute-start(bf16[96,8,1,48]{0,3,2,1:T(8,128)(2,1)} %get-tuple-element.60), channel_id=1, source_target_pairs={{0,16},{8,24},{16,32},{24,40},{32,48},{40,56},{48,64},{56,72},{64,... | collective-permute-start | bytes 221192 | tf_op jit(solution)/shard_map/ppermute | solution.py:21
  44.6 17.2 %collective-permute-start.3 = (bf16[96,8,1,48]{0,3,2,1:T(8,128)(2,1)}, bf16[96,8,1,48]{0,3,2,1:T(8,128)(2,1)}, u32[]{:S(2)}, u32[]{:S(2)}) collective-permute-start(bf16[96,8,1,48]{0,3,2,1:T(8,128)(2,1)} %get-tuple-element.61), channel_id=1, source_target_pairs={{16,0},{24,8},{32,16},{40,24},{48,32},{56,40},{64,48},{72,56},{80,... | collective-permute-start | bytes 221192 | tf_op jit(solution)/shard_map/ppermute | solution.py:21
  48.4 8.3 %collective-permute-start.6 = (f32[1,24,48]{2,1,0:T(8,128)S(1)}, f32[1,24,48]{2,1,0:T(8,128)S(1)}, u32[]{:S(2)}, u32[]{:S(2)}) collective-permute-start(f32[1,24,48]{2,1,0:T(8,128)S(1)} %get-tuple-element.86), channel_id=1, source_target_pairs={{0,64},{8,72},{16,80},{24,88},{32,96},{40,104},{48,112},{56,120},{... | collective-permute-start | bytes 13832 | tf_op jit(solution)/shard_map/ppermute | solution.py:21
  55.4 32.1 %copy-start.7 = (bf16[96,8,1,48]{0,3,2,1:T(8,128)(2,1)}, bf16[96,8,1,48]{0,3,2,1:T(8,128)(2,1)S(1)}, u32[]{:S(2)}) copy-start(bf16[96,8,1,48]{0,3,2,1:T(8,128)(2,1)S(1)} %broadcast_select_fusion.7) | copy-start | bytes 221188
  55.4 4.4 %collective-permute-start.7 = (f32[1,24,48]{2,1,0:T(8,128)S(1)}, f32[1,24,48]{2,1,0:T(8,128)S(1)}, u32[]{:S(2)}, u32[]{:S(2)}) collective-permute-start(f32[1,24,48]{2,1,0:T(8,128)S(1)} %get-tuple-element.87), channel_id=1, source_target_pairs={{64,0},{72,8},{80,16},{88,24},{96,32},{104,40},{112,48},{120,56},{... | collective-permute-start | bytes 13832 | tf_op jit(solution)/shard_map/ppermute | solution.py:21
  59.9 4.1 %collective-permute-start.8 = (f32[8,1,48]{2,1,0:T(1,128)S(1)}, f32[8,1,48]{2,1,0:T(1,128)S(1)}, u32[]{:S(2)}, u32[]{:S(2)}) collective-permute-start(f32[8,1,48]{2,1,0:T(1,128)S(1)} %get-tuple-element.84), channel_id=1, source_target_pairs={{0,16},{8,24},{16,32},{24,40},{32,48},{40,56},{48,64},{56,72},{64,... | collective-permute-start | bytes 4616 | tf_op jit(solution)/shard_map/ppermute | solution.py:21
  62.7 24.8 %copy-start.9 = (bf16[96,8,1,48]{0,3,2,1:T(8,128)(2,1)}, bf16[96,8,1,48]{0,3,2,1:T(8,128)(2,1)S(1)}, u32[]{:S(2)}) copy-start(bf16[96,8,1,48]{0,3,2,1:T(8,128)(2,1)S(1)} %broadcast_select_fusion.6) | copy-start | bytes 221188
  62.7 4.4 %collective-permute-start.9 = (f32[8,1,48]{2,1,0:T(1,128)S(1)}, f32[8,1,48]{2,1,0:T(1,128)S(1)}, u32[]{:S(2)}, u32[]{:S(2)}) collective-permute-start(f32[8,1,48]{2,1,0:T(1,128)S(1)} %get-tuple-element.85), channel_id=1, source_target_pairs={{16,0},{24,8},{32,16},{40,24},{48,32},{56,40},{64,48},{72,56},{80,... | collective-permute-start | bytes 4616 | tf_op jit(solution)/shard_map/ppermute | solution.py:21
  67.2 15.9 %collective-permute-start.10 = (f32[8,26,1]{2,1,0:T(8,128)S(1)}, f32[8,26,1]{2,1,0:T(8,128)S(1)}, u32[]{:S(2)}, u32[]{:S(2)}) collective-permute-start(f32[8,26,1]{2,1,0:T(8,128)S(1)} %get-tuple-element.82), channel_id=1, source_target_pairs={{0,8},{8,16},{16,24},{24,32},{32,40},{40,48},{48,56},{56,64},{64,7... | collective-permute-start | bytes 2504 | tf_op jit(solution)/shard_map/ppermute | solution.py:21
  76.1 17.4 %collective-permute-start.4 = (bf16[96,8,26,1]{0,3,2,1:T(2,128)(2,1)}, bf16[96,8,26,1]{0,3,2,1:T(2,128)(2,1)}, u32[]{:S(2)}, u32[]{:S(2)}) collective-permute-start(bf16[96,8,26,1]{0,3,2,1:T(2,128)(2,1)} %get-tuple-element.58), channel_id=1, source_target_pairs={{0,8},{8,16},{16,24},{24,32},{32,40},{40,48},{48,56},{56,64},{64,7... | collective-permute-start | bytes 119816 | tf_op jit(solution)/shard_map/ppermute | solution.py:21
  78.0 27.2 %collective-permute-start.5 = (bf16[96,8,26,1]{0,3,2,1:T(2,128)(2,1)}, bf16[96,8,26,1]{0,3,2,1:T(2,128)(2,1)}, u32[]{:S(2)}, u32[]{:S(2)}) collective-permute-start(bf16[96,8,26,1]{0,3,2,1:T(2,128)(2,1)} %get-tuple-element.59), channel_id=1, source_target_pairs={{8,0},{16,8},{24,16},{32,24},{40,32},{48,40},{56,48},{64,56},{72,6... | collective-permute-start | bytes 119816 | tf_op jit(solution)/shard_map/ppermute | solution.py:21
  81.0 6.3 %collective-permute-start.11 = (f32[8,26,1]{2,1,0:T(8,128)S(1)}, f32[8,26,1]{2,1,0:T(8,128)S(1)}, u32[]{:S(2)}, u32[]{:S(2)}) collective-permute-start(f32[8,26,1]{2,1,0:T(8,128)S(1)} %get-tuple-element.83), channel_id=1, source_target_pairs={{8,0},{16,8},{24,16},{32,24},{40,32},{48,40},{56,48},{64,56},{72,6... | collective-permute-start | bytes 2504 | tf_op jit(solution)/shard_map/ppermute | solution.py:21
  91.5 4.9 %collective-permute-start.12 = (bf16[2,5,48,96]{3,2,1,0:T(8,128)(2,1)S(1)}, bf16[2,5,48,96]{3,2,1,0:T(8,128)(2,1)S(1)}, u32[]{:S(2)}, u32[]{:S(2)}) collective-permute-start(bf16[2,5,48,96]{3,2,1,0:T(8,128)(2,1)S(1)} %get-tuple-element.70), channel_id=1, source_target_pairs={{0,64},{8,72},{16,80},{24,88},{32,96},{40,104},{48,112},{56,120},{... | collective-permute-start | bytes 276488 | tf_op jit(solution)/shard_map/ppermute | solution.py:21
  95.1 5.6 %collective-permute-start.13 = (bf16[2,5,48,96]{3,2,1,0:T(8,128)(2,1)S(1)}, bf16[2,5,48,96]{3,2,1,0:T(8,128)(2,1)S(1)}, u32[]{:S(2)}, u32[]{:S(2)}) collective-permute-start(bf16[2,5,48,96]{3,2,1,0:T(8,128)(2,1)S(1)} %get-tuple-element.71), channel_id=1, source_target_pairs={{64,0},{72,8},{80,16},{88,24},{96,32},{104,40},{112,48},{120,56},{... | collective-permute-start | bytes 276488 | tf_op jit(solution)/shard_map/ppermute | solution.py:21
  100.8 6.4 %collective-permute-start.14 = (bf16[2,22,5,96]{3,2,1,0:T(8,128)(2,1)S(1)}, bf16[2,22,5,96]{3,2,1,0:T(8,128)(2,1)S(1)}, u32[]{:S(2)}, u32[]{:S(2)}) collective-permute-start(bf16[2,22,5,96]{3,2,1,0:T(8,128)(2,1)S(1)} %get-tuple-element.66), channel_id=1, source_target_pairs={{0,16},{8,24},{16,32},{24,40},{32,48},{40,56},{48,64},{56,72},{64,... | collective-permute-start | bytes 126728 | tf_op jit(solution)/shard_map/ppermute | solution.py:21
  105.9 6.7 %collective-permute-start.15 = (bf16[2,22,5,96]{3,2,1,0:T(8,128)(2,1)S(1)}, bf16[2,22,5,96]{3,2,1,0:T(8,128)(2,1)S(1)}, u32[]{:S(2)}, u32[]{:S(2)}) collective-permute-start(bf16[2,22,5,96]{3,2,1,0:T(8,128)(2,1)S(1)} %get-tuple-element.67), channel_id=1, source_target_pairs={{16,0},{24,8},{32,16},{40,24},{48,32},{56,40},{64,48},{72,56},{80,... | collective-permute-start | bytes 126728 | tf_op jit(solution)/shard_map/ppermute | solution.py:21
  116.5 13.5 %collective-permute-start.16 = (bf16[2,22,58,5]{2,0,3,1:T(2,128)(2,1)}, bf16[2,22,58,5]{2,0,3,1:T(2,128)(2,1)}, u32[]{:S(2)}, u32[]{:S(2)}) collective-permute-start(bf16[2,22,58,5]{2,0,3,1:T(2,128)(2,1)} %copy.73), channel_id=1, source_target_pairs={{0,8},{8,16},{16,24},{24,32},{32,40},{40,48},{48,56},{56,64},{64,7... | collective-permute-start | bytes 76568 | tf_op jit(solution)/shard_map/ppermute | solution.py:21
  128.1 6.9 %collective-permute-start.17 = (bf16[2,22,58,5]{2,0,3,1:T(2,128)(2,1)S(1)}, bf16[2,22,58,5]{2,0,3,1:T(2,128)(2,1)S(1)}, u32[]{:S(2)}, u32[]{:S(2)}) collective-permute-start(bf16[2,22,58,5]{2,0,3,1:T(2,128)(2,1)S(1)} %copy.75), channel_id=1, source_target_pairs={{8,0},{16,8},{24,16},{32,24},{40,32},{48,40},{56,48},{64,56},{72,6... | collective-permute-start | bytes 76568 | tf_op jit(solution)/shard_map/ppermute | solution.py:21
  (11 other events, 72.2 us)
where the time goes:
time: 194 us; the launch traced here: 192 us
  starting transfers between devices  60.5 us (31%)
  local copies, waits for them, and re-layouts  60.4 us (31%)
  other arithmetic  36.7 us (19%)
  waiting for transfers between devices  20.3 us (10%)
  matrix products  12.2 us (6%)
    ppermute x18, starting transfers between devices, passed_along(): return lax.ppermute(block, axis, route)  52.3 us
    scatter x3, local copies, waits for them, and re-layouts, local(): extended = extended.at[1:-1, 1:-1, 1:-1].set(updated)  29.3 us
    ppermute x18, waiting for transfers between devices, passed_along(): return lax.ppermute(block, axis, route)  20 us
    dot_general x1, matrix products, local(): jnp.dot(occupations, squares, precision=precise).reshape(BX, BY, BZ)  12.2 us
    convert_element_type x1, other arithmetic, local(): (-0.5 * laplace + effective[None] * wave_field).astype(jnp.bfloat16)  10.2 us
    unnamed x39, local copies, waits for them, and re-layouts  8.39 us
    all_to_all x1, starting transfers between devices, sent_to_all(): lax.all_to_all(jnp.broadcast_to(x[None], (devices, *x.shape)), axis, 0, 0...  8.19 us
    select_n x4, other arithmetic, local(): updated = jnp.where(inside, (neighbour(extended) + wide_source) / 6.0, 0.0)  6.84 us
  transfers between devices with their start and end apart: 19, of which 6 were waited for; matrix products, arithmetic and copies ran while one was open for 24% of the time, Pallas kernels for 0%

commit v1 on v0

v1 whole, which is shorter than its diff:
```python
import functools
import math

import jax
import jax.numpy as jnp
from jax import lax
from jax.experimental import pallas as pl
from jax.experimental.pallas import tpu as pltpu
from jax.sharding import PartitionSpec as P

BX, BY, BZ = 6, 24, 48
YZ = BY * BZ
FX, FY, FZ = 2 * BX, 2 * BY, 2 * BZ
FYZ = FY * FZ
BANDS = 768
SWEEPS = 4
M = 5
NX = FX + 2 * M
YROWS = FY + 16
EDGE = 192
OWN = FX * 36
LANES = 128
MESH = pl.DeviceIdType.MESH
F32, BF16 = jnp.float32, jnp.bfloat16
EXACT = lax.Precision.HIGHEST

OFFSETS = [
    (dx, dy, dz) for dx in (-1, 0, 1) for dy in (-1, 0, 1) for dz in (0, 1) if (dx, dy, dz) != (0, 0, 0)
]


def slot_of(dx, dy, dz):
    return ((dx + 1) * 3 + dy + 1) * 2 + dz


HALO = 0
BAND = 18
ORB_X, ORB_Y, ORB_Z = 26, 28, 30
POT_X, POT_Y, POT_Z = 31, 35, 39
N_SEM = 41


def iota(shape, axis):
    return lax.broadcasted_iota(jnp.int32, shape, axis)


def step_kernel(
    sizes,
    orb, occ_in, prev_in, comp_in, loc_in,
    stencil, eff_out, pot_out,
    obuf, zbuf, ylo, yhi, w_ref, occ, occ_col,
    pvx, cmx, send_v, send_c, edge_v, edge_c, loc,
    va, vb, sa, vz, sz,
    part, gath, tot, totb, rh, xo, xz, cbuf, f1, f2, g3, c3, tmp_m,
    load_sem, send_sem, recv_sem,
):
    nb, n_band, nx, ny = sizes
    me = lax.axis_index("dom")
    band = lax.axis_index("band")
    bi = me // (ny * 2)
    bj = (me // 2) % ny
    bk = me % 2
    has_xlo, has_xhi = bi > 0, bi < nx - 1
    has_ylo, has_yhi = bj > 0, bj < ny - 1

    def exists(dx, dy):
        ok = None
        for flag in ([has_xlo] if dx < 0 else [has_xhi] if dx > 0 else []) + (
            [has_ylo] if dy < 0 else [has_yhi] if dy > 0 else []
        ):
            ok = flag if ok is None else jnp.logical_and(ok, flag)
        return ok

    def when(cond, fn):
        if cond is None:
            fn()
        else:
            pl.when(cond)(fn)

    def neighbour(dx, dy, dz):
        other = (1 - bk) if dz else bk
        return {"dom": ((bi + dx) * ny + bj + dy) * 2 + other, "band": band}

    def remote(src, dst, s_idx, r_idx, device):
        return pltpu.make_async_remote_copy(
            src_ref=src, dst_ref=dst, send_sem=send_sem.at[s_idx], recv_sem=recv_sem.at[r_idx],
            device_id=device, device_id_type=MESH,
        )

    cp_occ = pltpu.make_async_copy(occ_in, occ, load_sem.at[BX])
    cp_prev = pltpu.make_async_copy(prev_in, pvx.at[pl.ds(EDGE, OWN)], load_sem.at[BX + 1])
    cp_comp = pltpu.make_async_copy(comp_in, cmx.at[pl.ds(EDGE, OWN)], load_sem.at[BX + 2])
    cp_loc = pltpu.make_async_copy(loc_in, loc, load_sem.at[BX + 3])
    loads = [pltpu.make_async_copy(orb.at[x], obuf.at[x + 1], load_sem.at[x]) for x in range(BX)]
    cp_occ.start()
    cp_prev.start()
    cp_comp.start()
    for cp in loads:
        cp.start()
    cp_loc.start()

    barrier = pltpu.get_barrier_semaphore()
    for d in range(1, n_band):
        pl.semaphore_signal(
            barrier, inc=1, device_id={"dom": me, "band": (band + d) % n_band}, device_id_type=MESH
        )
    for dx, dy, dz in OFFSETS:
        def greet(dx=dx, dy=dy, dz=dz):
            pl.semaphore_signal(barrier, inc=1, device_id=neighbour(dx, dy, dz), device_id_type=MESH)
        when(exists(dx, dy), greet)

    def zero(ref, *index):
        def run():
            view = ref.at[index] if index else ref
            view[...] = jnp.zeros(view.shape, view.dtype)
        return run

    when(jnp.logical_not(has_xhi), zero(obuf, BX + 1))
    when(jnp.logical_not(has_xlo), zero(obuf, 0))
    for ref in (edge_v, edge_c):
        when(jnp.logical_not(has_xhi), zero(ref, 0))
        when(jnp.logical_not(has_xlo), zero(ref, 1))
    when(jnp.logical_not(has_ylo), zero(ylo))
    when(jnp.logical_not(has_yhi), zero(yhi))
    for dx, dy, dz in OFFSETS:
        cond = exists(dx, dy)
        if cond is not None:
            when(jnp.logical_not(cond), zero(rh, slot_of(dx, dy, dz)))
    for ref in (va, sa):
        when(jnp.logical_not(has_ylo), zero(ref, slice(None), pl.ds(0, 8)))
        when(jnp.logical_not(has_yhi), zero(ref, slice(None), pl.ds(8 + FY, 8)))
    for x in (0, NX - 1):
        vb[x] = jnp.zeros((YROWS, LANES), F32)
    cbuf[...] = jnp.zeros(cbuf.shape, F32)
    xo[...] = jnp.zeros(xo.shape, F32)
    xz[...] = jnp.zeros(xz.shape, F32)

    def fill_w(r, carry):
        row = iota((LANES, 384), 0) + r * LANES
        col = iota((LANES, 384), 1)
        place = col % BZ
        diff = row - LANES - col
        main = jnp.where(diff == 0, 3.0, 0.0)
        side = (
            (diff == BZ) | (diff == -BZ)
            | ((diff == 1) & (place != BZ - 1)) | ((diff == -1) & (place != 0))
        )
        main = jnp.where(side, -0.5, main)
        far = row - 640 - col
        over = jnp.where(
            bk == 0,
            jnp.where((far == 1 - BZ) & (place == BZ - 1), -0.5, 0.0),
            jnp.where((far == BZ - 1) & (place == 0), -0.5, 0.0),
        )
        w_ref[pl.ds(pl.multiple_of(r * LANES, LANES), LANES), :] = jnp.where(row < 640, main, over).astype(BF16)
        return carry

    lax.fori_loop(0, 8, fill_w, 0)

    cp_occ.wait()
    diagonal = jnp.where(iota((nb, nb), 0) == iota((nb, nb), 1), occ[...] * (1.0 / BANDS), 0.0)
    occ_col[...] = jnp.broadcast_to(jnp.sum(diagonal, 1, keepdims=True), (nb, LANES))

    cp_prev.wait()
    cp_comp.wait()
    send_v[...] = pvx[EDGE : EDGE + OWN, :].astype(BF16)
    send_c[...] = cmx[EDGE : EDGE + OWN, :].astype(BF16)

    one = lambda flag: jnp.where(flag, 1, 0)
    n_dom = (1 + one(has_xlo) + one(has_xhi)) * (1 + one(has_ylo) + one(has_yhi)) * 2 - 1
    pl.semaphore_wait(barrier, n_dom + n_band - 1)

    px_dn, px_up = [], []
    for n, (src, dst) in enumerate(((send_v, edge_v), (send_c, edge_c))):
        px_dn.append(remote(src.at[pl.ds(0, EDGE)], dst.at[0], POT_X + 2 * n, POT_X + 2 * n, neighbour(-1, 0, 0)))
        px_up.append(
            remote(
                src.at[pl.ds(OWN - EDGE, EDGE)], dst.at[1], POT_X + 2 * n + 1, POT_X + 2 * n + 1, neighbour(1, 0, 0)
            )
        )
    for cp in px_dn:
        when(has_xlo, cp.start)
    for cp in px_up:
        when(has_xhi, cp.start)

    oz = remote(orb, zbuf, ORB_Z, ORB_Z, neighbour(0, 0, 1))
    oz.start()
    oy_dn = remote(orb.at[:, :, pl.ds(0, LANES)], yhi, ORB_Y, ORB_Y, neighbour(0, -1, 0))
    oy_up = remote(orb.at[:, :, pl.ds(YZ - LANES, LANES)], ylo, ORB_Y + 1, ORB_Y + 1, neighbour(0, 1, 0))
    ox_dn = remote(orb.at[0], obuf.at[BX + 1], ORB_X, ORB_X, neighbour(-1, 0, 0))
    ox_up = remote(orb.at[BX - 1], obuf.at[0], ORB_X + 1, ORB_X + 1, neighbour(1, 0, 0))
    when(has_xlo, ox_dn.start)
    when(has_xhi, ox_up.start)
    when(has_ylo, oy_dn.start)
    when(has_yhi, oy_up.start)

    for x in range(BX):
        loads[x].wait()

        def body(g, acc, x=x):
            rows = pl.ds(pl.multiple_of(g * 16, 16), 16)
            share = occ_col[rows, :]
            out = []
            for blk in range(YZ // LANES):
                wave = obuf[x + 1, rows, LANES * blk : LANES * (blk + 1)].astype(F32)
                term = (wave * share) * wave
                out.append(acc[blk] + (term[0:8] + term[8:16]))
            return tuple(out)

        acc = lax.fori_loop(0, nb // 16, body, (jnp.zeros((8, LANES), F32),) * (YZ // LANES))
        for blk in range(YZ // LANES):
            part[x : x + 1, LANES * blk : LANES * (blk + 1)] = jnp.sum(acc[blk], 0, keepdims=True)
    part[BX:8, :] = jnp.zeros((8 - BX, YZ), F32)
    gath[band] = part[...].astype(BF16)
    band_copies = []
    for d in range(1, n_band):
        cp = remote(
            gath.at[band], gath.at[band], BAND + d, BAND + d, {"dom": me, "band": (band + d) % n_band}
        )
        cp.start()
        band_copies.append(cp)

    for cp in px_dn:
        when(has_xhi, cp.wait_recv)
    for cp in px_up:
        when(has_xlo, cp.wait_recv)
    for full, edge in ((pvx, edge_v), (cmx, edge_c)):
        full[EDGE + OWN : 2 * EDGE + OWN, :] = edge[0].astype(F32)
        full[0:EDGE, :] = edge[1].astype(F32)
    lane12 = iota((12, LANES), 1)

    def split(x, carry):
        base = EDGE - 36 * M + 36 * x
        for src, dst, scale in ((pvx, va, None), (cmx, sa, -math.pi)):
            a0, a1, a2 = (src[pl.ds(base + r, 12, stride=3), :] for r in range(3))
            if scale is not None:
                a0, a1, a2 = scale * a0, scale * a1, scale * a2
            cut = lane12 < FZ
            y0 = a0
            y1 = jnp.where(lane12 < 32, pltpu.roll(a0, 32, 1), pltpu.roll(a1, 32, 1))
            y2 = jnp.where(lane12 < 64, pltpu.roll(a1, 64, 1), pltpu.roll(a2, 64, 1))
            y3 = pltpu.roll(a2, 96, 1)
            for q, val in enumerate((y0, y1, y2, y3)):
                dst[x, pl.ds(8 + q, 12, stride=4), :] = jnp.where(cut, val, 0.0)
        return carry

    lax.fori_loop(0, NX, split, 0)
    y_copies = []
    for n, ref in enumerate((va, sa)):
        dn = remote(
            ref.at[:, pl.ds(8, 8)], ref.at[:, pl.ds(8 + FY, 8)], POT_Y + 2 * n, POT_Y + 2 * n, neighbour(0, -1, 0)
        )
        up = remote(
            ref.at[:, pl.ds(FY, 8)], ref.at[:, pl.ds(0, 8)], POT_Y + 2 * n + 1, POT_Y + 2 * n + 1, neighbour(0, 1, 0)
        )
        when(has_ylo, dn.start)
        when(has_yhi, up.start)
        y_copies.append((dn, up))
    for dn, up in y_copies:
        when(has_yhi, dn.wait_recv)
        when(has_ylo, up.wait_recv)
    z_copies = [
        remote(va, vz, POT_Z, POT_Z, neighbour(0, 0, 1)),
        remote(sa, sz, POT_Z + 1, POT_Z + 1, neighbour(0, 0, 1)),
    ]
    for cp in z_copies:
        cp.start()

    for cp in band_copies:
        cp.wait_recv()
    rho = gath[0].astype(F32)
    for d in range(1, n_band):
        rho = rho + gath[d].astype(F32)
    tot[...] = rho
    totb[...] = rho.astype(BF16)
    halo_copies = []
    for dx, dy, dz in OFFSETS:
        there = slot_of(-dx, -dy, dz)
        cols = {0: pl.ds(0, YZ), -1: pl.ds(0, 256), 1: pl.ds(YZ - 256, 256)}[dy]
        cp = remote(
            totb.at[:, cols], rh.at[there, :, cols], HALO + slot_of(dx, dy, dz), HALO + there,
            neighbour(dx, dy, dz),
        )
        when(exists(dx, dy), cp.start)
        halo_copies.append((dx, dy, cp))

    oz.wait_recv()
    when(has_yhi, oy_dn.wait_recv)
    when(has_ylo, oy_up.wait_recv)
    when(has_xhi, ox_dn.wait_recv)
    when(has_xlo, ox_up.wait_recv)

    def apply(x, carry):
        for t in range(3):
            if t == 0:
                here = [ylo[x], obuf[x + 1, :, 0:512]]
            elif t == 1:
                here = [obuf[x + 1, :, 256:896]]
            else:
                here = [obuf[x + 1, :, 640:1152], yhi[x]]
            lhs = jnp.concatenate([*here, zbuf[x, :, 384 * t : 384 * (t + 1)]], 1)
            out = jnp.dot(lhs, w_ref[...], preferred_element_type=F32)
            cols = slice(384 * t, 384 * (t + 1))
            sides = obuf[x, :, cols].astype(F32) + obuf[x + 2, :, cols].astype(F32)
            stencil[x, :, cols] = out - 0.5 * sides
        return carry

    lax.fori_loop(0, BX, apply, 0)

    for cp in z_copies:
        cp.wait_recv()
        cp.wait_send()
    for dn, up in y_copies:
        when(has_ylo, dn.wait_send)
        when(has_yhi, up.wait_send)
    lane = iota((YROWS, LANES), 1)
    from_z = jnp.where(bk == 0, jnp.where((lane >= FZ) & (lane < FZ + M), 1, 0), jnp.where(lane >= LANES - M, 1, 0)) == 1
    shift = FZ - 64 * bk

    def merge(x, carry):
        va[x] = jnp.where(from_z, pltpu.roll(vz[x], shift, 1), va[x])
        sa[x] = jnp.where(from_z, pltpu.roll(sz[x], shift, 1), sa[x])
        return carry

    lax.fori_loop(0, NX, merge, 0)

    for dx, dy, cp in halo_copies:
        when(exists(-dx, -dy), cp.wait_recv)
    for dst, dz in ((xo, 0), (xz, 1)):
        for dy, start, width, at in ((0, 0, YZ, 256), (-1, YZ - 256, 256, 0), (1, 0, 256, 256 + YZ)):
            cols = slice(start, start + width)
            own = tot[...] if dz == 0 and dy == 0 else rh[slot_of(0, dy, dz), :, cols].astype(F32)
            above = rh[slot_of(1, dy, dz), :, cols].astype(F32)
            below = rh[slot_of(-1, dy, dz), :, cols].astype(F32)
            lanes = slice(at, at + width)
            dst[0:3, lanes] = below[3:6]
            dst[3:9, lanes] = own[0:6]
            dst[9:12, lanes] = above[0:3]

    def split_rho(g, carry):
        window = pl.ds(pl.multiple_of(g * 384, 384), 512)
        for src, base in ((xo, 0), (xz, 64)):
            block = src[:, window]
            for q in range(8):
                cbuf[g * 8 + q, :, base : base + BZ] = block[:, 112 + BZ * q : 112 + BZ * (q + 1)]
        return carry

    lax.fori_loop(0, 4, split_rho, 0)
    source_row = iota((LANES, LANES), 0)
    fine_lane = iota((LANES, LANES), 1)
    fine_z = jnp.where(fine_lane >= LANES - M, fine_lane - LANES, fine_lane)
    coarse = jnp.where(source_row < 64, source_row, source_row - 64 + jnp.where(bk == 0, BZ, -BZ))
    real = (source_row < BZ) | ((source_row >= 64) & (source_row < 64 + BZ))
    odd = (fine_z + 128) % 2
    half = (fine_z + 128) // 2 - 64
    wz = jnp.where(coarse == half, 0.75 * math.pi, 0.0)
    wz = jnp.where(coarse == half - 1 + 2 * odd, 0.25 * math.pi, wz)
    wz = jnp.where(real, wz, 0.0)
    fine = jnp.dot(
        cbuf[...].reshape(32 * 16, LANES), wz, precision=EXACT, preferred_element_type=F32
    ).reshape(32, 16, LANES)
    for y in range(30):
        f1[pl.ds(y + 5, 12, stride=40), :] = fine[y, 0:12]

    def refine_y(x, carry):
        base = pl.multiple_of(x * 40, 8)
        block = f1[pl.ds(base, 40), :]
        mid = 0.75 * block[6:34]
        f2[x, pl.ds(4, 28, stride=2), :] = mid + 0.25 * block[5:33]
        f2[x, pl.ds(5, 28, stride=2), :] = mid + 0.25 * block[7:35]
        return carry

    lax.fori_loop(0, 12, refine_y, 0)

    def refine_x(x, carry):
        mid = 0.75 * f2[x]
        at = 2 * x - 1
        sa[at] = sa[at] + mid + 0.25 * f2[x - 1]
        sa[at + 1] = sa[at + 1] + mid + 0.25 * f2[x + 1]
        return carry

    lax.fori_loop(1, 11, refine_x, 0)

    yrow = iota((YROWS, LANES), 0)
    y_ok = ((yrow >= 8) | has_ylo) & ((yrow < 8 + FY) | has_yhi)
    z_ok = (lane < FZ) | from_z
    sixth = jnp.where(y_ok & z_ok, 1.0 / 6.0, 0.0)
    x_low = jnp.where(has_xlo, 1.0, 0.0)
    x_high = jnp.where(has_xhi, 1.0, 0.0)

    for sweep in range(SWEEPS):
        old, new = (va, vb) if sweep % 2 == 0 else (vb, va)

        def update(x, carry, old=old, new=new):
            mid = old[x]
            acc = old[x - 1] + old[x + 1] + sa[x]
            acc = acc + pltpu.roll(mid, 1, 0) + pltpu.roll(mid, YROWS - 1, 0)
            acc = acc + pltpu.roll(mid, 1, 1) + pltpu.roll(mid, LANES - 1, 1)
            factor = jnp.where(x < M, x_low, jnp.where(x >= M + FX, x_high, 1.0))
            new[x] = acc * (sixth * factor)
            return carry

        lax.fori_loop(1 + sweep, NX - 1 - sweep, update, 0)

    def coarsen(x, carry):
        at = 2 * x + M
        g3[...] = 0.125 * (va[at - 1] + va[at + 2]) + 0.375 * (va[at] + va[at + 1])
        c3[pl.ds(pl.multiple_of(x * BY, 8), BY), :] = 0.125 * (
            g3[pl.ds(7, BY, stride=2), :] + g3[pl.ds(10, BY, stride=2), :]
        ) + 0.375 * (g3[pl.ds(8, BY, stride=2), :] + g3[pl.ds(9, BY, stride=2), :])
        return carry

    lax.fori_loop(0, BX, coarsen, 0)
    lane_in = iota((LANES, LANES), 0)
    cell = iota((LANES, LANES), 1)
    rel = jnp.where(lane_in == LANES - 1, -1, lane_in) - 2 * cell
    wr = jnp.where((rel == 0) | (rel == 1), 0.375, 0.0)
    wr = jnp.where((rel == -1) | (rel == 2), 0.125, wr)
    wr = jnp.where(cell < BZ, wr, 0.0)
    c3[...] = jnp.dot(c3[...], wr, precision=EXACT, preferred_element_type=F32)
    cp_loc.wait()
    for y in range(BY):
        tmp_m[0:BX, y * BZ : (y + 1) * BZ] = c3[pl.ds(y, BX, stride=BY), :][:, 0:BZ]
    for x in range(BX):
        cube = jnp.exp(jnp.log((3.0 / math.pi) * tot[x : x + 1, :]) * (1.0 / 3.0))
        eff_out[x : x + 1, :] = (tmp_m[x : x + 1, :] - cube) + loc[x]

    def join(x, carry):
        p0, p1, p2, p3 = (va[x + M, pl.ds(8 + q, 12, stride=4), :] for q in range(4))
        r0 = jnp.where(lane12 < 96, p0, pltpu.roll(p1, 96, 1))
        r1 = jnp.where(lane12 < 64, pltpu.roll(p1, 96, 1), pltpu.roll(p2, 64, 1))
        r2 = jnp.where(lane12 < 32, pltpu.roll(p2, 64, 1), pltpu.roll(p3, 32, 1))
        for r, val in enumerate((r0, r1, r2)):
            pot_out[pl.ds(36 * x + r, 12, stride=3), :] = val
        return carry

    lax.fori_loop(0, FX, join, 0)

    for cp in px_dn:
        when(has_xlo, cp.wait_send)
    for cp in px_up:
        when(has_xhi, cp.wait_send)
    oz.wait_send()
    when(has_ylo, oy_dn.wait_send)
    when(has_yhi, oy_up.wait_send)
    when(has_xlo, ox_dn.wait_send)
    when(has_xhi, ox_up.wait_send)
    for cp in band_copies:
        cp.wait_send()
    for dx, dy, cp in halo_copies:
        when(exists(dx, dy), cp.wait_send)


def solution(mesh):
    n_band = mesh.shape["band"]
    domains = mesh.shape["dom"]
    ny = min(4, domains // 4)
    nx = domains // (ny * 2)

    def local(orbitals, occupations, previous, compensation, local_potential):
        nb = orbitals.shape[0]
        any_space = pl.BlockSpec(memory_space=pl.ANY)
        vmem = pl.BlockSpec(memory_space=pltpu.VMEM)
        waves = orbitals[:, 0].transpose(1, 0, 2)
        stencil, effective, potential = pl.pallas_call(
            functools.partial(step_kernel, (nb, n_band, nx, ny)),
            out_shape=(
                jax.ShapeDtypeStruct((BX, nb, YZ), F32),
                jax.ShapeDtypeStruct((BX, YZ), F32),
                jax.ShapeDtypeStruct((OWN, LANES), F32),
            ),
            in_specs=[any_space] * 5,
            out_specs=(vmem, vmem, vmem),
            scratch_shapes=[
                pltpu.VMEM((BX + 2, nb, YZ), BF16),
                pltpu.VMEM((BX, nb, YZ), BF16),
                pltpu.VMEM((BX, nb, LANES), BF16),
                pltpu.VMEM((BX, nb, LANES), BF16),
                pltpu.VMEM((1024, 384), BF16),
                pltpu.VMEM((1, nb), F32),
                pltpu.VMEM((nb, LANES), F32),
                pltpu.VMEM((2 * EDGE + OWN, LANES), F32),
                pltpu.VMEM((2 * EDGE + OWN, LANES), F32),
                pltpu.VMEM((OWN, LANES), BF16),
                pltpu.VMEM((OWN, LANES), BF16),
                pltpu.VMEM((2, EDGE, LANES), BF16),
                pltpu.VMEM((2, EDGE, LANES), BF16),
                pltpu.VMEM((BX, 1, YZ), F32),
            ]
            + [pltpu.VMEM((NX, YROWS, LANES), F32)] * 5
            + [
                pltpu.VMEM((8, YZ), F32),
                pltpu.VMEM((n_band, 8, YZ), BF16),
                pltpu.VMEM((8, YZ), F32),
                pltpu.VMEM((8, YZ), BF16),
                pltpu.VMEM((18, 8, YZ), BF16),
                pltpu.VMEM((16, 512 + YZ), F32),
                pltpu.VMEM((16, 512 + YZ), F32),
                pltpu.VMEM((32, 16, LANES), F32),
                pltpu.VMEM((12 * 40, LANES), F32),
                pltpu.VMEM((12, YROWS, LANES), F32),
                pltpu.VMEM((YROWS, LANES), F32),
                pltpu.VMEM((BX * BY, LANES), F32),
                pltpu.VMEM((8, YZ), F32),
                pltpu.SemaphoreType.DMA((BX + 4,)),
                pltpu.SemaphoreType.DMA((N_SEM,)),
                pltpu.SemaphoreType.DMA((N_SEM,)),
            ],
            compiler_params=pltpu.CompilerParams(
                collective_id=0, has_side_effects=True, vmem_limit_bytes=48 * 1024 * 1024
            ),
        )(
            waves,
            occupations.reshape(1, nb),
            previous.reshape(OWN, LANES),
            compensation.reshape(OWN, LANES),
            local_potential.reshape(BX, 1, YZ),
        )
        applied = (stencil + effective[:, None] * waves.astype(F32)).astype(BF16)
        return applied.transpose(1, 0, 2)[:, None], potential.reshape(previous.shape)

    return jax.shard_map(
        local,
        mesh=mesh,
        in_specs=(
            P("band", "dom", None, None),
            P("band"),
            P("dom", None, None),
            P("dom", None, None),
            P("dom", None, None),
        ),
        out_specs=(P("band", "dom", None, None), P("dom", None, None)),
        check_vma=False,
    )
```

time: 194 us -> 44.7 us (0.23); the launches traced: 192 us -> 44.5 us
  starting transfers between devices: 60.5 us -> 0 us
  local copies, waits for them, and re-layouts: 60.4 us -> 5.27 us
  Pallas kernels: 0 us -> 37.2 us
  other arithmetic: 36.7 us -> 1.38 us
  waiting for transfers between devices: 20.3 us -> 0 us
  matrix products: 12.2 us -> 0 us
    ppermute x18 -> x0, starting transfers between devices: 52.3 us -> none  [passed_along(): return lax.ppermute(block, axis, route)]
    pallas_call x0 -> x1, Pallas kernels: none -> 37.2 us  [local(): pl.pallas_call(functools.partial(step_kernel, (nb, n_band, nx, ny)), out_...]
    scatter x3 -> x0, local copies, waits for them, and re-layouts: 29.3 us -> none  [local(): extended = extended.at[1:-1, 1:-1, 1:-1].set(updated)]
    ppermute x18 -> x0, waiting for transfers between devices: 20 us -> none  [passed_along(): return lax.ppermute(block, axis, route)]
    convert_element_type x2 -> x0, other arithmetic: 16.2 us -> none  [the longest x1 10.2 us: local(): (-0.5 * laplace + effective[None] * wave_field).astype(jnp.bfloat16)]
    select_n x22 -> x0, other arithmetic: 13.2 us -> none  [the longest x4 6.84 us: local(): updated = jnp.where(inside, (neighbour(extended) + wide_source) / 6.0, 0.0)]
    dot_general x1 -> x0, matrix products: 12.2 us -> none  [local(): jnp.dot(occupations, squares, precision=precise).reshape(BX, BY, BZ)]
    slice x21 -> x0, local copies, waits for them, and re-layouts: 9.28 us -> none  [the longest x5 4.53 us: extend(): upper_rim = lax.slice_in_dim(array_in, length - width, length, axis=along)]
  transfers between devices with their start and end apart: 19 -> 0, of which waited for: 6 -> 0; matrix products, arithmetic and copies ran while one was open for 24% -> 0% of each run, Pallas kernels for 0% -> 0%
where the time goes in v1:
time: 44.7 us; the launch traced here: 44.5 us
  Pallas kernels  37.2 us (83%)
  local copies, waits for them, and re-layouts  5.27 us (12%)
  other arithmetic  1.38 us (3%)
  between operations  0.65 us (1%)
    pallas_call x1, Pallas kernels, local(): pl.pallas_call(functools.partial(step_kernel, (nb, n_band, nx, ny)), out_...  37.2 us
    unnamed x11, local copies, waits for them, and re-layouts  5.27 us
    broadcast_in_dim x1, other arithmetic, local(): applied.transpose(1, 0, 2)[:, None]  1.38 us

profile of v1, /device:TPU:1, one launch (start us, length us, event | category | flops | bytes accessed | tf_op | source)
XLA Modules:
  0.0 44.5 jit_solution(1735375583083669748)
XLA Ops:
  0.6 0.0 copy-start
  0.6 1.3 %copy-done = bf16[96,1,6,1152]{3,0,2,1:T(8,128)(2,1)S(1)} copy-done((bf16[96,1,6,1152]{3,0,2,1:T(8,128)(2,1)S(1)}, bf16[96,1,6,1152]{3,0,2,1:T(8,128)(2,1)}, u32[]{:S(2)}) %copy-start) | copy-done | bytes 1327128
  2.0 0.0 copy-start.1
  2.0 0.9 %copy-done.1 = f32[1,12,4608]{2,0,1:T(1,128)S(1)} copy-done((f32[1,12,4608]{2,0,1:T(1,128)S(1)}, f32[1,12,4608]{2,0,1:T(1,128)}, u32[]{:S(2)}) %copy-start.1) | copy-done | bytes 221208
  2.9 0.0 copy-start.2
  2.9 0.9 %copy-done.2 = f32[1,12,4608]{2,0,1:T(1,128)S(1)} copy-done((f32[1,12,4608]{2,0,1:T(1,128)S(1)}, f32[1,12,4608]{2,0,1:T(1,128)}, u32[]{:S(2)}) %copy-start.2) | copy-done | bytes 221208
  3.8 0.0 copy-start.3
  3.8 0.7 %copy-done.3 = f32[1,6,1152]{2,0,1:T(1,128)S(1)} copy-done((f32[1,6,1152]{2,0,1:T(1,128)S(1)}, f32[1,6,1152]{2,0,1:T(1,128)}, u32[]{:S(2)}) %copy-start.3) | copy-done | bytes 27672
  4.6 0.0 copy-start.4
  4.6 0.7 %copy-done.4 = f32[96]{0:T(128)S(1)} copy-done((f32[96]{0:T(128)S(1)}, f32[96]{0:T(128)}, u32[]{:S(2)}) %copy-start.4) | copy-done | bytes 408
  5.2 37.2 %shard_map.68 = (f32[6,96,1152]{2,1,0:T(8,128)S(1)}, f32[6,1152]{1,0:T(8,128)S(1)}, f32[432,128]{1,0:T(8,128)S(1)}) custom-call(bf16[6,96,1152]{2,1,0:T(8,128)(2,1)S(1)} %bitcast.13, f32[1,96]{1,0:T(1,128)S(1)} %bitcast.18, f32[432,128]{1,0:T(8,128)S(1)} %bitcast.15, f32[432,128]{1,0:T(8,128)S(1)} %bitcast.16, f32[6,1,1152]{2,1,0:T(1,128)S(1)} %bitcast.17), custom_call_target="tpu_custom_call" | custom-call | tf_op jit(solution)/shard_map/pallas_call | solution.py:465
  42.4 1.4 %fusion = bf16[96,1,6,1152]{3,0,2,1:T(8,128)(2,1)} fusion(f32[6,96,1152]{2,1,0:T(8,128)S(1)} %get-tuple-element.5, f32[6,1152]{1,0:T(8,128)S(1)} %get-tuple-element.6, bf16[96,1,6,1152]{3,0,2,1:T(8,128)(2,1)S(1)} %copy-done), kind=kLoop, calls=%fused_computation.1 | loop fusion | flops 2654208 | bytes 5336064 | tf_op jit(solution)/shard_map/broadcast_in_dim | solution.py:520
  43.8 0.7 %copy.10 = f32[1,12,4608]{2,0,1:T(1,128)} copy(f32[1,12,4608]{2,0,1:T(1,128)S(1)} %bitcast.14) | data formatting | bytes 442368
Async XLA Ops:
  0.6 1.3 %copy-start = (bf16[96,1,6,1152]{3,0,2,1:T(8,128)(2,1)S(1)}, bf16[96,1,6,1152]{3,0,2,1:T(8,128)(2,1)}, u32[]{:S(2)}) copy-start(bf16[96,1,6,1152]{3,0,2,1:T(8,128)(2,1)} %param.5) | copy-start | bytes 3981316
  2.0 0.9 %copy-start.1 = (f32[1,12,4608]{2,0,1:T(1,128)S(1)}, f32[1,12,4608]{2,0,1:T(1,128)}, u32[]{:S(2)}) copy-start(f32[1,12,4608]{2,0,1:T(1,128)} %param.7) | copy-start | bytes 663556
  2.9 0.9 %copy-start.2 = (f32[1,12,4608]{2,0,1:T(1,128)S(1)}, f32[1,12,4608]{2,0,1:T(1,128)}, u32[]{:S(2)}) copy-start(f32[1,12,4608]{2,0,1:T(1,128)} %param.8) | copy-start | bytes 663556
  3.8 0.7 %copy-start.3 = (f32[1,6,1152]{2,0,1:T(1,128)S(1)}, f32[1,6,1152]{2,0,1:T(1,128)}, u32[]{:S(2)}) copy-start(f32[1,6,1152]{2,0,1:T(1,128)} %param.9) | copy-start | bytes 82948
  4.6 0.7 %copy-start.4 = (f32[96]{0:T(128)S(1)}, f32[96]{0:T(128)}, u32[]{:S(2)}) copy-start(f32[96]{0:T(128)} %param.6) | copy-start | bytes 1156

commit v2 on v1

v2 whole, which is shorter than its diff:
```python
import functools
import math

import jax
import jax.numpy as jnp
from jax import lax
from jax.experimental import pallas as pl
from jax.experimental.pallas import tpu as pltpu
from jax.sharding import PartitionSpec as P

BX, BY, BZ = 6, 24, 48
YZ = BY * BZ
FX, FY, FZ = 2 * BX, 2 * BY, 2 * BZ
FYZ = FY * FZ
BANDS = 768
SWEEPS = 4
M = 5
NX = FX + 2 * M
Y0 = 16
YROWS = FY + 2 * Y0
SPAN = FY + 16
EDGE = 192
OWN = FX * 36
LANES = 128
MESH = pl.DeviceIdType.MESH
F32, BF16 = jnp.float32, jnp.bfloat16
EXACT = lax.Precision.HIGHEST

OFFSETS = [
    (dx, dy, dz) for dx in (-1, 0, 1) for dy in (-1, 0, 1) for dz in (0, 1) if (dx, dy, dz) != (0, 0, 0)
]


def slot_of(dx, dy, dz):
    return ((dx + 1) * 3 + dy + 1) * 2 + dz


HALO = 0
BAND = 18
ORB_X, ORB_Y, ORB_Z = 26, 28, 30
POT_X, POT_Y, POT_Z = 31, 35, 39
N_SEM = 41


def loop(low, high, body, together):
    def some(step, carry):
        for u in range(together):
            body(low + step * together + u)
        return carry

    assert (high - low) % together == 0
    lax.fori_loop(0, (high - low) // together, some, 0)


def iota(shape, axis):
    return lax.broadcasted_iota(jnp.int32, shape, axis)


def step_kernel(
    sizes,
    orb, occ_in, prev_in, comp_in, loc_in,
    stencil, eff_out, pot_out, waves,
    xlo, xhi, zbuf, ylo, yhi, w_ref, occ, occ_col,
    pvx, cmx, send_v, send_c, edge_v, edge_c, loc,
    va, vb, sa, rim_out, rim_in, zsend, zrecv,
    part, gath, tot, totb, rh, xo, xz, cbuf, f1, f2, g3, c3, tmp_m, base,
    load_sem, send_sem, recv_sem,
):
    nb, n_band, nx, ny = sizes
    me = lax.axis_index("dom")
    band = lax.axis_index("band")
    bi = me // (ny * 2)
    bj = (me // 2) % ny
    bk = me % 2
    has_xlo, has_xhi = bi > 0, bi < nx - 1
    has_ylo, has_yhi = bj > 0, bj < ny - 1

    def exists(dx, dy):
        ok = None
        for flag in ([has_xlo] if dx < 0 else [has_xhi] if dx > 0 else []) + (
            [has_ylo] if dy < 0 else [has_yhi] if dy > 0 else []
        ):
            ok = flag if ok is None else jnp.logical_and(ok, flag)
        return ok

    def when(cond, fn):
        if cond is None:
            fn()
        else:
            pl.when(cond)(fn)

    def neighbour(dx, dy, dz):
        other = (1 - bk) if dz else bk
        return {"dom": ((bi + dx) * ny + bj + dy) * 2 + other, "band": band}

    def remote(src, dst, s_idx, r_idx, device):
        return pltpu.make_async_remote_copy(
            src_ref=src, dst_ref=dst, send_sem=send_sem.at[s_idx], recv_sem=recv_sem.at[r_idx],
            device_id=device, device_id_type=MESH,
        )

    leftovers = []

    def send(cp, where, arrival):
        when(where, cp.start)
        handle = [cp, arrival, False]
        leftovers.append((handle, where))
        return handle

    def arrive(*handles):
        for handle in handles:
            when(handle[1], handle[0].wait_recv)
            handle[2] = True

    def finish():
        for handle, where in leftovers:
            if not handle[2]:
                arrive(handle)
            when(where, handle[0].wait_send)

    cp_occ = pltpu.make_async_copy(occ_in, occ, load_sem.at[BX])
    cp_prev = pltpu.make_async_copy(prev_in, pvx.at[pl.ds(EDGE, OWN)], load_sem.at[BX + 1])
    cp_comp = pltpu.make_async_copy(comp_in, cmx.at[pl.ds(EDGE, OWN)], load_sem.at[BX + 2])
    cp_loc = pltpu.make_async_copy(loc_in, loc, load_sem.at[BX + 3])
    loads = [pltpu.make_async_copy(orb.at[x], waves.at[x], load_sem.at[x]) for x in range(BX)]
    cp_occ.start()
    for cp in loads:
        cp.start()
    cp_prev.start()
    cp_comp.start()
    cp_loc.start()

    barrier = pltpu.get_barrier_semaphore()
    for d in range(1, n_band):
        pl.semaphore_signal(
            barrier, inc=1, device_id={"dom": me, "band": (band + d) % n_band}, device_id_type=MESH
        )
    for dx, dy, dz in OFFSETS:
        def greet(dx=dx, dy=dy, dz=dz):
            pl.semaphore_signal(barrier, inc=1, device_id=neighbour(dx, dy, dz), device_id_type=MESH)
        when(exists(dx, dy), greet)

    cp_occ.wait()
    diagonal = jnp.where(iota((nb, nb), 0) == iota((nb, nb), 1), occ[...] * (1.0 / BANDS), 0.0)
    occ_col[...] = jnp.broadcast_to(jnp.sum(diagonal, 1, keepdims=True), (nb, LANES))

    part[...] = jnp.zeros((8, YZ), F32)
    base[...] = jnp.zeros((8, YZ), F32)
    for x in range(BX):
        loads[x].wait()

        for blk in range(YZ // LANES):
            cols = slice(LANES * blk, LANES * (blk + 1))
            wave = waves[x, :, cols].astype(F32)
            part[x : x + 1, cols] = jnp.sum((wave * occ_col[...]) * wave, 0, keepdims=True)

    def packed(field):
        mean = (jnp.sum(field, 0, keepdims=True) * (1.0 / BX)).astype(BF16).astype(F32)
        row = iota(field.shape, 0)
        return jnp.where(row < BX, field - mean, jnp.where(row == BX, mean, 0.0)).astype(BF16)

    def unpacked(block):
        return block + block[BX : BX + 1]

    gath[band] = packed(part[...])

    one = lambda flag: jnp.where(flag, 1, 0)
    n_dom = (1 + one(has_xlo) + one(has_xhi)) * (1 + one(has_ylo) + one(has_yhi)) * 2 - 1
    pl.semaphore_wait(barrier, n_dom + n_band - 1)
    band_in = [
        send(
            remote(gath.at[band], gath.at[band], BAND + d, BAND + d, {"dom": me, "band": (band + d) % n_band}),
            None, None,
        )
        for d in range(1, n_band)
    ]

    cp_prev.wait()
    cp_comp.wait()
    cp_loc.wait()
    send_v[...] = pvx[EDGE : EDGE + OWN, :].astype(BF16)
    send_c[...] = cmx[EDGE : EDGE + OWN, :].astype(BF16)
    px_in = []
    for n, (src, dst) in enumerate(((send_v, edge_v), (send_c, edge_c))):
        px_in.append(send(
            remote(src.at[pl.ds(0, EDGE)], dst.at[0], POT_X + 2 * n, POT_X + 2 * n, neighbour(-1, 0, 0)),
            has_xlo, has_xhi,
        ))
        px_in.append(send(
            remote(
                src.at[pl.ds(OWN - EDGE, EDGE)], dst.at[1], POT_X + 2 * n + 1, POT_X + 2 * n + 1, neighbour(1, 0, 0)
            ),
            has_xhi, has_xlo,
        ))

    orb_in = [
        send(remote(orb.at[0], xhi, ORB_X, ORB_X, neighbour(-1, 0, 0)), has_xlo, has_xhi),
        send(remote(orb.at[BX - 1], xlo, ORB_X + 1, ORB_X + 1, neighbour(1, 0, 0)), has_xhi, has_xlo),
        send(
            remote(orb.at[:, :, pl.ds(0, LANES)], yhi, ORB_Y, ORB_Y, neighbour(0, -1, 0)), has_ylo, has_yhi
        ),
        send(
            remote(orb.at[:, :, pl.ds(YZ - LANES, LANES)], ylo, ORB_Y + 1, ORB_Y + 1, neighbour(0, 1, 0)),
            has_yhi, has_ylo,
        ),
        send(remote(orb, zbuf, ORB_Z, ORB_Z, neighbour(0, 0, 1)), None, None),
    ]

    def zero(ref, *index):
        def run():
            view = ref.at[index] if index else ref
            view[...] = jnp.zeros(view.shape, view.dtype)
        return run

    when(jnp.logical_not(has_xhi), zero(xhi))
    when(jnp.logical_not(has_xlo), zero(xlo))
    for ref in (edge_v, edge_c):
        when(jnp.logical_not(has_xhi), zero(ref, 0))
        when(jnp.logical_not(has_xlo), zero(ref, 1))
    when(jnp.logical_not(has_ylo), zero(ylo))
    when(jnp.logical_not(has_yhi), zero(yhi))
    for dx, dy, dz in OFFSETS:
        cond = exists(dx, dy)
        if cond is not None:
            when(jnp.logical_not(cond), zero(rh, slot_of(dx, dy, dz)))
    when(jnp.logical_not(has_yhi), zero(rim_in, 0))
    when(jnp.logical_not(has_ylo), zero(rim_in, 1))
    for x in range(NX):
        for ref in (va, vb):
            ref[x, 0:8, :] = jnp.zeros((8, LANES), F32)
            ref[x, Y0 + FY + 8 :, :] = jnp.zeros((8, LANES), F32)
    cbuf[...] = jnp.zeros(cbuf.shape, F32)
    xo[...] = jnp.zeros(xo.shape, F32)
    xz[...] = jnp.zeros(xz.shape, F32)

    def fill_w(r, carry):
        row = iota((LANES, 384), 0) + r * LANES
        col = iota((LANES, 384), 1)
        place = iota((1, 384), 1) % BZ
        diff = row - LANES - col
        main = jnp.where(diff == 0, 3.0, 0.0)
        side = (
            (diff == BZ) | (diff == -BZ)
            | ((diff == 1) & (place != BZ - 1)) | ((diff == -1) & (place != 0))
        )
        main = jnp.where(side, -0.5, main)
        far = row - 640 - col
        over = jnp.where(
            bk == 0,
            jnp.where((far == 1 - BZ) & (place == BZ - 1), -0.5, 0.0),
            jnp.where((far == BZ - 1) & (place == 0), -0.5, 0.0),
        )
        w_ref[pl.ds(pl.multiple_of(r * LANES, LANES), LANES), :] = jnp.where(row < 640, main, over).astype(BF16)
        return carry

    lax.fori_loop(0, 8, fill_w, 0)

    arrive(*px_in)
    for full, edge in ((pvx, edge_v), (cmx, edge_c)):
        full[EDGE + OWN : 2 * EDGE + OWN, :] = edge[0].astype(F32)
        full[0:EDGE, :] = edge[1].astype(F32)
    lane12 = iota((12, LANES), 1)

    def split(x):
        base = EDGE - 36 * M + 36 * x
        for n, (src, dst, scale) in enumerate(((pvx, va, None), (cmx, sa, -math.pi))):
            a0, a1, a2 = (src[pl.ds(base + r, 12, stride=3), :] for r in range(3))
            if scale is not None:
                a0, a1, a2 = scale * a0, scale * a1, scale * a2
            cut = lane12 < FZ
            y0 = a0
            y1 = jnp.where(lane12 < 32, pltpu.roll(a0, 32, 1), pltpu.roll(a1, 32, 1))
            y2 = jnp.where(lane12 < 64, pltpu.roll(a1, 64, 1), pltpu.roll(a2, 64, 1))
            y3 = pltpu.roll(a2, 96, 1)
            for q, val in enumerate((y0, y1, y2, y3)):
                dst[x, pl.ds(Y0 + q, 12, stride=4), :] = jnp.where(cut, val, 0.0)
            rim_out[0, n, x] = dst[x, Y0 : Y0 + 8, :].astype(BF16)
            rim_out[1, n, x] = dst[x, Y0 + FY - 8 : Y0 + FY, :].astype(BF16)

    loop(0, NX, split, 2)
    rim_copies = [
        send(remote(rim_out.at[0], rim_in.at[0], POT_Y, POT_Y, neighbour(0, -1, 0)), has_ylo, has_yhi),
        send(remote(rim_out.at[1], rim_in.at[1], POT_Y + 1, POT_Y + 1, neighbour(0, 1, 0)), has_yhi, has_ylo),
    ]

    arrive(*band_in)
    rho = gath[0].astype(F32)
    for d in range(1, n_band):
        rho = rho + gath[d].astype(F32)
    rho = jnp.where(iota((8, YZ), 0) < BX, unpacked(rho), 0.0)
    tot[...] = rho
    totb[...] = packed(rho)
    halo_in = []
    for dx, dy, dz in OFFSETS:
        there = slot_of(-dx, -dy, dz)
        cols = {0: pl.ds(0, YZ), -1: pl.ds(0, 256), 1: pl.ds(YZ - 256, 256)}[dy]
        cp = remote(
            totb.at[:, cols], rh.at[there, :, cols], HALO + slot_of(dx, dy, dz), HALO + there,
            neighbour(dx, dy, dz),
        )
        halo_in.append(send(cp, exists(dx, dy), exists(-dx, -dy)))

    for x in range(BX):
        base[x : x + 1, :] = loc[x]
    base[...] = base[...] - jnp.exp(jnp.log((3.0 / math.pi) * tot[...]) * (1.0 / 3.0))

    arrive(*rim_copies)
    lane = iota((SPAN, LANES), 1)
    span = slice(Y0 - 8, Y0 - 8 + SPAN)
    inner = (lane < M) | ((lane >= 64) & (lane < 64 + M))

    def pack_z(x):
        for n, ref in enumerate((va, sa)):
            ref[x, Y0 + FY : Y0 + FY + 8, :] = rim_in[0, n, x].astype(F32)
            ref[x, Y0 - 8 : Y0, :] = rim_in[1, n, x].astype(F32)
        v, s = va[x, span, :], sa[x, span, :]
        first = jnp.where(lane < 64, v, pltpu.roll(s, 64, 1))
        last = jnp.where(lane < 64, pltpu.roll(v, 16 + M - FZ + LANES, 1), pltpu.roll(s, 80 + M - FZ + LANES, 1))
        zsend[x] = jnp.where(inner, first, last).astype(BF16)

    loop(0, NX, pack_z, 2)
    z_in = send(remote(zsend, zrecv, POT_Z, POT_Z, neighbour(0, 0, 1)), None, None)

    arrive(*orb_in)

    for x in range(BX):
        for t in range(3):
            if t == 0:
                here = [ylo[x], waves[x, :, 0:512]]
            elif t == 1:
                here = [waves[x, :, 256:896]]
            else:
                here = [waves[x, :, 640:1152], yhi[x]]
            cols = slice(384 * t, 384 * (t + 1))
            lhs = jnp.concatenate([*here, zbuf[x, :, cols]], 1)
            out = jnp.dot(lhs, w_ref[...], preferred_element_type=F32)
            below = xlo[:, cols] if x == 0 else waves[x - 1, :, cols]
            above = xhi[:, cols] if x == BX - 1 else waves[x + 1, :, cols]
            stencil[x, :, cols] = out - 0.5 * (below.astype(F32) + above.astype(F32))

    arrive(z_in)
    from_z = jnp.where(bk == 0, jnp.where((lane >= FZ) & (lane < FZ + M), 1, 0), jnp.where(lane >= LANES - M, 1, 0)) == 1
    shift_v = jnp.where(bk == 0, FZ, LANES - M - 16)
    shift_s = jnp.where(bk == 0, FZ - 64, 64 - M - 16)

    def merge(x):
        rim = zrecv[x].astype(F32)
        va[x, span, :] = jnp.where(from_z, pltpu.roll(rim, shift_v, 1), va[x, span, :])
        sa[x, span, :] = jnp.where(from_z, pltpu.roll(rim, shift_s, 1), sa[x, span, :])

    loop(0, NX, merge, 2)

    arrive(*halo_in)
    for dst, dz in ((xo, 0), (xz, 1)):
        for dy, start, width, at in ((0, 0, YZ, 256), (-1, YZ - 256, 256, 0), (1, 0, 256, 256 + YZ)):
            cols = slice(start, start + width)
            own = tot[...] if dz == 0 and dy == 0 else unpacked(rh[slot_of(0, dy, dz), :, cols].astype(F32))
            above = unpacked(rh[slot_of(1, dy, dz), :, cols].astype(F32))
            below = unpacked(rh[slot_of(-1, dy, dz), :, cols].astype(F32))
            lanes = slice(at, at + width)
            dst[0:3, lanes] = below[3:6]
            dst[3:9, lanes] = own[0:6]
            dst[9:12, lanes] = above[0:3]

    def split_rho(g):
        window = pl.ds(pl.multiple_of(g * 384, 384), 512)
        for src, base in ((xo, 0), (xz, 64)):
            block = src[:, window]
            for q in range(8):
                cbuf[g * 8 + q, :, base : base + BZ] = block[:, 112 + BZ * q : 112 + BZ * (q + 1)]

    loop(0, 4, split_rho, 2)
    source_row = iota((LANES, LANES), 0)
    fine_lane = iota((LANES, LANES), 1)
    fine_z = jnp.where(fine_lane >= LANES - M, fine_lane - LANES, fine_lane)
    coarse = jnp.where(source_row < 64, source_row, source_row - 64 + jnp.where(bk == 0, BZ, -BZ))
    real = (source_row < BZ) | ((source_row >= 64) & (source_row < 64 + BZ))
    odd = (fine_z + 128) % 2
    half = (fine_z + 128) // 2 - 64
    wz = jnp.where(coarse == half, 0.75 * math.pi, 0.0)
    wz = jnp.where(coarse == half - 1 + 2 * odd, 0.25 * math.pi, wz)
    wz = jnp.where(real, wz, 0.0)
    fine = jnp.dot(
        cbuf[...].reshape(32 * 16, LANES), wz, precision=EXACT, preferred_element_type=F32
    ).reshape(32, 16, LANES)
    for y in range(30):
        f1[pl.ds(y + 5, 12, stride=40), :] = fine[y, 0:12]

    def refine_y(x):
        base = pl.multiple_of(x * 40, 8)
        block = f1[pl.ds(base, 40), :]
        mid = 0.75 * block[6:34]
        f2[x, pl.ds(4, 28, stride=2), :] = mid + 0.25 * block[5:33]
        f2[x, pl.ds(5, 28, stride=2), :] = mid + 0.25 * block[7:35]

    loop(0, 12, refine_y, 4)

    def refine_x(x):
        mid = 0.75 * f2[x]
        at = 2 * x - 1
        sa[at, span, :] = sa[at, span, :] + mid + 0.25 * f2[x - 1]
        sa[at + 1, span, :] = sa[at + 1, span, :] + mid + 0.25 * f2[x + 1]

    loop(1, 11, refine_x, 5)

    yrow = iota((SPAN, LANES), 0)
    y_ok = ((yrow >= 8) | has_ylo) & ((yrow < 8 + FY) | has_yhi)
    z_ok = (lane < FZ) | from_z
    sixth = jnp.where(y_ok & z_ok, 1.0 / 6.0, 0.0)
    x_low = jnp.where(has_xlo, 1.0, 0.0)
    x_high = jnp.where(has_xhi, 1.0, 0.0)

    for sweep in range(SWEEPS):
        old, new = (va, vb) if sweep % 2 == 0 else (vb, va)

        def update(x, old=old, new=new):
            mid = old[x, span, :]
            acc = old[x - 1, span, :] + old[x + 1, span, :] + sa[x, span, :]
            acc = acc + (old[x, Y0 - 9 : Y0 - 9 + SPAN, :] + old[x, Y0 - 7 : Y0 - 7 + SPAN, :])
            acc = acc + pltpu.roll(mid, 1, 1) + pltpu.roll(mid, LANES - 1, 1)
            factor = jnp.where(x < M, x_low, jnp.where(x >= M + FX, x_high, 1.0))
            new[x, span, :] = acc * (sixth * factor)

        loop(1 + sweep, NX - 1 - sweep, update, (5, 6, 4, 7)[sweep])

    for x in range(BX):
        at = 2 * x + M
        g3[x, 0:YROWS, :] = 0.125 * (va[at - 1] + va[at + 2]) + 0.375 * (va[at] + va[at + 1])
    for x in range(BX):
        c3[BY * x : BY * (x + 1), :] = 0.125 * (
            g3[x, pl.ds(Y0 - 1, BY, stride=2), :] + g3[x, pl.ds(Y0 + 2, BY, stride=2), :]
        ) + 0.375 * (g3[x, pl.ds(Y0, BY, stride=2), :] + g3[x, pl.ds(Y0 + 1, BY, stride=2), :])
    lane_in = iota((LANES, LANES), 0)
    cell = iota((LANES, LANES), 1)
    rel = jnp.where(lane_in == LANES - 1, -1, lane_in) - 2 * cell
    wr = jnp.where((rel == 0) | (rel == 1), 0.375, 0.0)
    wr = jnp.where((rel == -1) | (rel == 2), 0.125, wr)
    wr = jnp.where(cell < BZ, wr, 0.0)
    c3[...] = jnp.dot(c3[...], wr, precision=EXACT, preferred_element_type=F32)
    for y in range(BY):
        tmp_m[0:BX, y * BZ : (y + 1) * BZ] = c3[pl.ds(y, BX, stride=BY), :][:, 0:BZ]
    eff_out[...] = tmp_m[0:BX, :] + base[0:BX, :]

    def join(x):
        p0, p1, p2, p3 = (va[x + M, pl.ds(Y0 + q, 12, stride=4), :] for q in range(4))
        r0 = jnp.where(lane12 < 96, p0, pltpu.roll(p1, 96, 1))
        r1 = jnp.where(lane12 < 64, pltpu.roll(p1, 96, 1), pltpu.roll(p2, 64, 1))
        r2 = jnp.where(lane12 < 32, pltpu.roll(p2, 64, 1), pltpu.roll(p3, 32, 1))
        for r, val in enumerate((r0, r1, r2)):
            pot_out[pl.ds(36 * x + r, 12, stride=3), :] = val

    loop(0, FX, join, 6)

    finish()


def solution(mesh):
    n_band = mesh.shape["band"]
    domains = mesh.shape["dom"]
    ny = min(4, domains // 4)
    nx = domains // (ny * 2)

    def local(orbitals, occupations, previous, compensation, local_potential):
        nb = orbitals.shape[0]
        hbm = pl.BlockSpec(memory_space=pltpu.HBM)
        vmem = pl.BlockSpec(memory_space=pltpu.VMEM)
        waves = orbitals[:, 0].transpose(1, 0, 2)
        stencil, effective, potential, held = pl.pallas_call(
            functools.partial(step_kernel, (nb, n_band, nx, ny)),
            out_shape=(
                jax.ShapeDtypeStruct((BX, nb, YZ), F32),
                jax.ShapeDtypeStruct((BX, YZ), F32),
                jax.ShapeDtypeStruct((OWN, LANES), F32),
                jax.ShapeDtypeStruct((BX, nb, YZ), BF16),
            ),
            in_specs=[hbm] * 5,
            out_specs=(vmem,) * 4,
            scratch_shapes=[
                pltpu.VMEM((nb, YZ), BF16),
                pltpu.VMEM((nb, YZ), BF16),
                pltpu.VMEM((BX, nb, YZ), BF16),
                pltpu.VMEM((BX, nb, LANES), BF16),
                pltpu.VMEM((BX, nb, LANES), BF16),
                pltpu.VMEM((1024, 384), BF16),
                pltpu.VMEM((1, nb), F32),
                pltpu.VMEM((nb, LANES), F32),
                pltpu.VMEM((2 * EDGE + OWN, LANES), F32),
                pltpu.VMEM((2 * EDGE + OWN, LANES), F32),
                pltpu.VMEM((OWN, LANES), BF16),
                pltpu.VMEM((OWN, LANES), BF16),
                pltpu.VMEM((2, EDGE, LANES), BF16),
                pltpu.VMEM((2, EDGE, LANES), BF16),
                pltpu.VMEM((BX, 1, YZ), F32),
            ]
            + [pltpu.VMEM((NX, YROWS, LANES), F32)] * 3
            + [
                pltpu.VMEM((2, 2, NX, 8, LANES), BF16),
                pltpu.VMEM((2, 2, NX, 8, LANES), BF16),
                pltpu.VMEM((NX, SPAN, LANES), BF16),
                pltpu.VMEM((NX, SPAN, LANES), BF16),
                pltpu.VMEM((8, YZ), F32),
                pltpu.VMEM((n_band, 8, YZ), BF16),
                pltpu.VMEM((8, YZ), F32),
                pltpu.VMEM((8, YZ), BF16),
                pltpu.VMEM((18, 8, YZ), BF16),
                pltpu.VMEM((16, 512 + YZ), F32),
                pltpu.VMEM((16, 512 + YZ), F32),
                pltpu.VMEM((32, 16, LANES), F32),
                pltpu.VMEM((12 * 40, LANES), F32),
                pltpu.VMEM((12, SPAN, LANES), F32),
                pltpu.VMEM((BX, YROWS, LANES), F32),
                pltpu.VMEM((BX * BY, LANES), F32),
                pltpu.VMEM((8, YZ), F32),
                pltpu.VMEM((8, YZ), F32),
                pltpu.SemaphoreType.DMA((BX + 4,)),
                pltpu.SemaphoreType.DMA((N_SEM,)),
                pltpu.SemaphoreType.DMA((N_SEM,)),
            ],
            compiler_params=pltpu.CompilerParams(
                collective_id=0, has_side_effects=True, vmem_limit_bytes=48 * 1024 * 1024
            ),
        )(
            pltpu.with_memory_space_constraint(waves, pltpu.HBM),
            pltpu.with_memory_space_constraint(occupations.reshape(1, nb), pltpu.HBM),
            pltpu.with_memory_space_constraint(previous.reshape(OWN, LANES), pltpu.HBM),
            pltpu.with_memory_space_constraint(compensation.reshape(OWN, LANES), pltpu.HBM),
            pltpu.with_memory_space_constraint(local_potential.reshape(BX, 1, YZ), pltpu.HBM),
        )
        applied = (stencil + effective[:, None] * held.astype(F32)).astype(BF16)
        return applied.transpose(1, 0, 2)[:, None], potential.reshape(previous.shape)

    return jax.shard_map(
        local,
        mesh=mesh,
        in_specs=(
            P("band", "dom", None, None),
            P("band"),
            P("dom", None, None),
            P("dom", None, None),
            P("dom", None, None),
        ),
        out_specs=(P("band", "dom", None, None), P("dom", None, None)),
        check_vma=False,
    )
```

time: 44.7 us -> 30.2 us (0.68)
  Pallas kernels: 37.2 us -> 27.2 us
  local copies, waits for them, and re-layouts: 5.27 us -> 0.68 us
    pallas_call x1, Pallas kernels: 37.2 us -> 27.2 us  [local(): pl.pallas_call(functools.partial(step_kernel, (nb, n_band, nx, ny)), out_...]
    unnamed x11 -> x1, local copies, waits for them, and re-layouts: 5.27 us -> 0.68 us
where the time goes in v2:
time: 30.2 us; the launch traced here: 30 us
  Pallas kernels  27.2 us (90%)
  other arithmetic  1.48 us (5%)
  local copies, waits for them, and re-layouts  0.68 us (2%)
  between operations  0.64 us (2%)
    pallas_call x1, Pallas kernels, local(): pl.pallas_call(functools.partial(step_kernel, (nb, n_band, nx, ny)), out_...  27.2 us
    broadcast_in_dim x1, other arithmetic, local(): applied.transpose(1, 0, 2)[:, None]  1.48 us
    unnamed x1, local copies, waits for them, and re-layouts  0.68 us

profile of v2, /device:TPU:1, one launch (start us, length us, event | category | flops | bytes accessed | tf_op | source)
XLA Modules:
  0.0 30.0 jit_solution(11859111956667394572)
XLA Ops:
  0.6 27.2 %shard_map.68 = (f32[6,96,1152]{2,1,0:T(8,128)S(1)}, f32[6,1152]{1,0:T(8,128)S(1)}, f32[432,128]{1,0:T(8,128)S(1)}, bf16[6,96,1152]{2,1,0:T(8,128)(2,1)S(1)}) custom-call(bf16[6,96,1152]{2,1,0:T(8,128)(2,1)} %bitcast.13, f32[1,96]{1,0:T(1,128)} %bitcast.17, f32[432,128]{1,0:T(8,128)} %bitcast.14, f32[432,128]{1,0:T(8,128)} %bitcast.15, f32[6,1,1152]{2,1,0:T(1,128)} %bitcast.16), custom_call_target="tpu_custom_call" | custom-call | tf_op jit(solution)/shard_map/pallas_call | solution.py:468
  27.9 1.5 %fusion = bf16[96,1,6,1152]{3,0,2,1:T(8,128)(2,1)} fusion(f32[6,96,1152]{2,1,0:T(8,128)S(1)} %get-tuple-element.6, bf16[6,96,1152]{2,1,0:T(8,128)(2,1)S(1)} %get-tuple-element.8, f32[6,1152]{1,0:T(8,128)S(1)} %get-tuple-element.7), kind=kLoop, calls=%fused_computation.1 | loop fusion | flops 2654208 | bytes 5336064 | tf_op jit(solution)/shard_map/broadcast_in_dim | solution.py:530
  29.4 0.7 %copy.10 = f32[1,12,4608]{2,0,1:T(1,128)} copy(f32[1,12,4608]{2,0,1:T(1,128)S(1)} %bitcast.12) | data formatting | bytes 442368

commit v3 on v2

--- a/solution.py
+++ b/solution.py
@@ -37,9 +37,9 @@
 
 HALO = 0
 BAND = 18
-ORB_X, ORB_Y, ORB_Z = 26, 28, 30
-POT_X, POT_Y, POT_Z = 31, 35, 39
-N_SEM = 41
+ORB_X, ORB_Y, ORB_Z = 26, 30, 32
+POT_X, POT_Y, POT_Z = 33, 37, 43
+N_SEM = 44
 
 
 def loop(low, high, body, together):
@@ -62,7 +62,7 @@
     stencil, eff_out, pot_out, waves,
     xlo, xhi, zbuf, ylo, yhi, w_ref, occ, occ_col,
     pvx, cmx, send_v, send_c, edge_v, edge_c, loc,
-    va, vb, sa, rim_out, rim_in, zsend, zrecv,
+    va, vb, sa, rim_tmp, rim_out, rim_in, rim_all, zsend, zrecv,
     part, gath, tot, totb, rh, xo, xz, cbuf, f1, f2, g3, c3, tmp_m, base,
     load_sem, send_sem, recv_sem,
 ):
@@ -193,9 +193,39 @@
             has_xhi, has_xlo,
         ))
 
+    for x in range(FX):
+        for n, src in enumerate((pvx, cmx)):
+            at = EDGE + 36 * x
+            rim_tmp[0, n, 4 * x : 4 * x + 4, :] = src[at : at + 4, :]
+            rim_tmp[1, n, 4 * x : 4 * x + 4, :] = src[at + 32 : at + 36, :]
+    rim_out[...] = rim_tmp[...].astype(BF16)
+    rim_copies = []
+    for side, dy in ((0, -1), (1, 1)):
+        for dx in (0, -1, 1):
+            rows = {0: pl.ds(0, 48), -1: pl.ds(0, 32), 1: pl.ds(16, 32)}[dx]
+            cp = remote(
+                rim_out.at[side, :, rows], rim_in.at[1 - dx, side, :, rows],
+                POT_Y + 3 * side + dx + 1, POT_Y + 3 * side + dx + 1, neighbour(dx, dy, 0),
+            )
+            rim_copies.append(send(cp, exists(dx, dy), exists(-dx, -dy)))
+
+    half = pl.ds(0, nb // 2), pl.ds(nb // 2, nb // 2)
+
+    def orbitals_along_x(n):
+        return [
+            send(
+                remote(orb.at[0, half[n]], xhi.at[half[n]], ORB_X + 2 * n, ORB_X + 2 * n, neighbour(-1, 0, 0)),
+                has_xlo, has_xhi,
+            ),
+            send(
+                remote(
+                    orb.at[BX - 1, half[n]], xlo.at[half[n]], ORB_X + 2 * n + 1, ORB_X + 2 * n + 1, neighbour(1, 0, 0)
+                ),
+                has_xhi, has_xlo,
+            ),
+        ]
+
     orb_in = [
-        send(remote(orb.at[0], xhi, ORB_X, ORB_X, neighbour(-1, 0, 0)), has_xlo, has_xhi),
-        send(remote(orb.at[BX - 1], xlo, ORB_X + 1, ORB_X + 1, neighbour(1, 0, 0)), has_xhi, has_xlo),
         send(
             remote(orb.at[:, :, pl.ds(0, LANES)], yhi, ORB_Y, ORB_Y, neighbour(0, -1, 0)), has_ylo, has_yhi
         ),
@@ -205,6 +235,7 @@
         ),
         send(remote(orb, zbuf, ORB_Z, ORB_Z, neighbour(0, 0, 1)), None, None),
     ]
+    orb_x_in = orbitals_along_x(0)
 
     def zero(ref, *index):
         def run():
@@ -223,12 +254,13 @@
         cond = exists(dx, dy)
         if cond is not None:
             when(jnp.logical_not(cond), zero(rh, slot_of(dx, dy, dz)))
-    when(jnp.logical_not(has_yhi), zero(rim_in, 0))
-    when(jnp.logical_not(has_ylo), zero(rim_in, 1))
+    for side, dy in ((0, -1), (1, 1)):
+        for dx in (-1, 0, 1):
+            when(jnp.logical_not(exists(-dx, -dy)), zero(rim_in, 1 - dx, side))
     for x in range(NX):
-        for ref in (va, vb):
-            ref[x, 0:8, :] = jnp.zeros((8, LANES), F32)
-            ref[x, Y0 + FY + 8 :, :] = jnp.zeros((8, LANES), F32)
+        for ref in (va, vb, sa):
+            ref[x, 0:Y0, :] = jnp.zeros((Y0, LANES), F32)
+            ref[x, Y0 + FY :, :] = jnp.zeros((Y0, LANES), F32)
     cbuf[...] = jnp.zeros(cbuf.shape, F32)
     xo[...] = jnp.zeros(xo.shape, F32)
     xz[...] = jnp.zeros(xz.shape, F32)
@@ -255,33 +287,25 @@
 
     lax.fori_loop(0, 8, fill_w, 0)
 
-    arrive(*px_in)
-    for full, edge in ((pvx, edge_v), (cmx, edge_c)):
-        full[EDGE + OWN : 2 * EDGE + OWN, :] = edge[0].astype(F32)
-        full[0:EDGE, :] = edge[1].astype(F32)
     lane12 = iota((12, LANES), 1)
+
+    def thread(a0, a1, a2, lanes):
+        y0 = a0
+        y1 = jnp.where(lanes < 32, pltpu.roll(a0, 32, 1), pltpu.roll(a1, 32, 1))
+        y2 = jnp.where(lanes < 64, pltpu.roll(a1, 64, 1), pltpu.roll(a2, 64, 1))
+        y3 = pltpu.roll(a2, 96, 1)
+        return [jnp.where(lanes < FZ, val, 0.0) for val in (y0, y1, y2, y3)]
+
+    fields = ((pvx, va, 1.0), (cmx, sa, -math.pi))
 
     def split(x):
         base = EDGE - 36 * M + 36 * x
-        for n, (src, dst, scale) in enumerate(((pvx, va, None), (cmx, sa, -math.pi))):
-            a0, a1, a2 = (src[pl.ds(base + r, 12, stride=3), :] for r in range(3))
-            if scale is not None:
-                a0, a1, a2 = scale * a0, scale * a1, scale * a2
-            cut = lane12 < FZ
-            y0 = a0
-            y1 = jnp.where(lane12 < 32, pltpu.roll(a0, 32, 1), pltpu.roll(a1, 32, 1))
-            y2 = jnp.where(lane12 < 64, pltpu.roll(a1, 64, 1), pltpu.roll(a2, 64, 1))
-            y3 = pltpu.roll(a2, 96, 1)
-            for q, val in enumerate((y0, y1, y2, y3)):
-                dst[x, pl.ds(Y0 + q, 12, stride=4), :] = jnp.where(cut, val, 0.0)
-            rim_out[0, n, x] = dst[x, Y0 : Y0 + 8, :].astype(BF16)
-            rim_out[1, n, x] = dst[x, Y0 + FY - 8 : Y0 + FY, :].astype(BF16)
-
-    loop(0, NX, split, 2)
-    rim_copies = [
-        send(remote(rim_out.at[0], rim_in.at[0], POT_Y, POT_Y, neighbour(0, -1, 0)), has_ylo, has_yhi),
-        send(remote(rim_out.at[1], rim_in.at[1], POT_Y + 1, POT_Y + 1, neighbour(0, 1, 0)), has_yhi, has_ylo),
-    ]
+        for src, dst, scale in fields:
+            rows = [scale * src[pl.ds(base + r, 12, stride=3), :] for r in range(3)]
+            for q, val in enumerate(thread(*rows, lane12)):
+                dst[x, pl.ds(Y0 + q, 12, stride=4), :] = val
+
+    loop(M, M + FX, split, 6)
 
     arrive(*band_in)
     rho = gath[0].astype(F32)
@@ -300,19 +324,40 @@
         )
         halo_in.append(send(cp, exists(dx, dy), exists(-dx, -dy)))
 
-    for x in range(BX):
-        base[x : x + 1, :] = loc[x]
-    base[...] = base[...] - jnp.exp(jnp.log((3.0 / math.pi) * tot[...]) * (1.0 / 3.0))
-
+    orb_x_in = orb_x_in + orbitals_along_x(1)
+
+    arrive(*px_in)
+    for full, edge in ((pvx, edge_v), (cmx, edge_c)):
+        full[EDGE + OWN : 2 * EDGE + OWN, :] = edge[0].astype(F32)
+        full[0:EDGE, :] = edge[1].astype(F32)
+    loop(0, M, split, 5)
+    loop(M + FX, NX, split, 5)
     arrive(*rim_copies)
+    lane22 = iota((NX, LANES), 1)
+    for n, (_, dst, scale) in enumerate(fields):
+        flat = dst.reshape(NX * YROWS, LANES)
+        for side in range(2):
+            rim_tmp[0, 0, 0:20, :] = rim_in[0, side, n].astype(F32)[28:48]
+            rim_tmp[0, 0, 20:48, :] = rim_in[1, side, n].astype(F32)[0:28]
+            rim_tmp[0, 1, 0:20, :] = rim_in[1, side, n].astype(F32)[28:48]
+            rim_tmp[0, 1, 20:40, :] = rim_in[2, side, n].astype(F32)[0:20]
+            rim_all[side, n, 0:48, :] = rim_tmp[0, 0]
+            rim_all[side, n, 48:88, :] = rim_tmp[0, 1, 0:40, :]
+            a = [scale * rim_all[side, n, pl.ds(r, NX, stride=4), :] for r in range(4)]
+            if side == 0:
+                cells = [*thread(a[0], a[1], a[2], lane22), jnp.where(lane22 < FZ, a[3], 0.0)]
+                first = Y0 + FY
+            else:
+                cells = [jnp.where(lane22 < FZ, pltpu.roll(a[0], 96, 1), 0.0), *thread(a[1], a[2], a[3], lane22)]
+                first = Y0 - M
+            for q, val in enumerate(cells):
+                flat[pl.ds(first + q, NX, stride=YROWS), :] = val
+
     lane = iota((SPAN, LANES), 1)
     span = slice(Y0 - 8, Y0 - 8 + SPAN)
     inner = (lane < M) | ((lane >= 64) & (lane < 64 + M))
 
     def pack_z(x):
-        for n, ref in enumerate((va, sa)):
-            ref[x, Y0 + FY : Y0 + FY + 8, :] = rim_in[0, n, x].astype(F32)
-            ref[x, Y0 - 8 : Y0, :] = rim_in[1, n, x].astype(F32)
         v, s = va[x, span, :], sa[x, span, :]
         first = jnp.where(lane < 64, v, pltpu.roll(s, 64, 1))
         last = jnp.where(lane < 64, pltpu.roll(v, 16 + M - FZ + LANES, 1), pltpu.roll(s, 80 + M - FZ + LANES, 1))
@@ -321,9 +366,11 @@
     loop(0, NX, pack_z, 2)
     z_in = send(remote(zsend, zrecv, POT_Z, POT_Z, neighbour(0, 0, 1)), None, None)
 
-    arrive(*orb_in)
-
     for x in range(BX):
+        base[x : x + 1, :] = loc[x]
+    base[...] = base[...] - jnp.exp(jnp.log((3.0 / math.pi) * tot[...]) * (1.0 / 3.0))
+
+    def stencil_of(x):
         for t in range(3):
             if t == 0:
                 here = [ylo[x], waves[x, :, 0:512]]
@@ -338,6 +385,10 @@
             above = xhi[:, cols] if x == BX - 1 else waves[x + 1, :, cols]
             stencil[x, :, cols] = out - 0.5 * (below.astype(F32) + above.astype(F32))
 
+    arrive(*orb_in)
+    for x in range(1, BX - 1):
+        stencil_of(x)
+
     arrive(z_in)
     from_z = jnp.where(bk == 0, jnp.where((lane >= FZ) & (lane < FZ + M), 1, 0), jnp.where(lane >= LANES - M, 1, 0)) == 1
     shift_v = jnp.where(bk == 0, FZ, LANES - M - 16)
@@ -349,6 +400,10 @@
         sa[x, span, :] = jnp.where(from_z, pltpu.roll(rim, shift_s, 1), sa[x, span, :])
 
     loop(0, NX, merge, 2)
+
+    arrive(*orb_x_in)
+    stencil_of(0)
+    stencil_of(BX - 1)
 
     arrive(*halo_in)
     for dst, dz in ((xo, 0), (xz, 1)):
@@ -376,9 +431,9 @@
     coarse = jnp.where(source_row < 64, source_row, source_row - 64 + jnp.where(bk == 0, BZ, -BZ))
     real = (source_row < BZ) | ((source_row >= 64) & (source_row < 64 + BZ))
     odd = (fine_z + 128) % 2
-    half = (fine_z + 128) // 2 - 64
-    wz = jnp.where(coarse == half, 0.75 * math.pi, 0.0)
-    wz = jnp.where(coarse == half - 1 + 2 * odd, 0.25 * math.pi, wz)
+    floor = (fine_z + 128) // 2 - 64
+    wz = jnp.where(coarse == floor, 0.75 * math.pi, 0.0)
+    wz = jnp.where(coarse == floor - 1 + 2 * odd, 0.25 * math.pi, wz)
     wz = jnp.where(real, wz, 0.0)
     fine = jnp.dot(
         cbuf[...].reshape(32 * 16, LANES), wz, precision=EXACT, preferred_element_type=F32
@@ -494,8 +549,10 @@
             ]
             + [pltpu.VMEM((NX, YROWS, LANES), F32)] * 3
             + [
-                pltpu.VMEM((2, 2, NX, 8, LANES), BF16),
-                pltpu.VMEM((2, 2, NX, 8, LANES), BF16),
+                pltpu.VMEM((2, 2, 48, LANES), F32),
+                pltpu.VMEM((2, 2, 48, LANES), BF16),
+                pltpu.VMEM((3, 2, 2, 48, LANES), BF16),
+                pltpu.VMEM((2, 2, 88, LANES), F32),
                 pltpu.VMEM((NX, SPAN, LANES), BF16),
                 pltpu.VMEM((NX, SPAN, LANES), BF16),
                 pltpu.VMEM((8, YZ), F32),

time: 30.2 us -> 27.1 us (0.90)
  Pallas kernels: 27.2 us -> 24.2 us
    pallas_call x1, Pallas kernels: 27.2 us -> 24.2 us  [local(): pl.pallas_call(functools.partial(step_kernel, (nb, n_band, nx, ny)), out_...]
where the time goes in v3:
time: 27.1 us; the launch traced here: 27 us
  Pallas kernels  24.2 us (89%)
  other arithmetic  1.48 us (5%)
  local copies, waits for them, and re-layouts  0.68 us (3%)
  between operations  0.64 us (2%)
    pallas_call x1, Pallas kernels, local(): pl.pallas_call(functools.partial(step_kernel, (nb, n_band, nx, ny)), out_...  24.2 us
    broadcast_in_dim x1, other arithmetic, local(): applied.transpose(1, 0, 2)[:, None]  1.48 us
    unnamed x1, local copies, waits for them, and re-layouts  0.68 us

profile of v3, /device:TPU:1, one launch (start us, length us, event | category | flops | bytes accessed | tf_op | source)
XLA Modules:
  0.0 27.0 jit_solution(17935639062305701897)
XLA Ops:
  0.6 24.2 %shard_map.68 = (f32[6,96,1152]{2,1,0:T(8,128)S(1)}, f32[6,1152]{1,0:T(8,128)S(1)}, f32[432,128]{1,0:T(8,128)S(1)}, bf16[6,96,1152]{2,1,0:T(8,128)(2,1)S(1)}) custom-call(bf16[6,96,1152]{2,1,0:T(8,128)(2,1)} %bitcast.13, f32[1,96]{1,0:T(1,128)} %bitcast.17, f32[432,128]{1,0:T(8,128)} %bitcast.14, f32[432,128]{1,0:T(8,128)} %bitcast.15, f32[6,1,1152]{2,1,0:T(1,128)} %bitcast.16), custom_call_target="tpu_custom_call" | custom-call | tf_op jit(solution)/shard_map/pallas_call | solution.py:523
  24.8 1.5 %fusion = bf16[96,1,6,1152]{3,0,2,1:T(8,128)(2,1)} fusion(f32[6,96,1152]{2,1,0:T(8,128)S(1)} %get-tuple-element.6, bf16[6,96,1152]{2,1,0:T(8,128)(2,1)S(1)} %get-tuple-element.8, f32[6,1152]{1,0:T(8,128)S(1)} %get-tuple-element.7), kind=kLoop, calls=%fused_computation.1 | loop fusion | flops 2654208 | bytes 5336064 | tf_op jit(solution)/shard_map/broadcast_in_dim | solution.py:587
  26.3 0.7 %copy.10 = f32[1,12,4608]{2,0,1:T(1,128)} copy(f32[1,12,4608]{2,0,1:T(1,128)S(1)} %bitcast.12) | data formatting | bytes 442368

commit v4 on v3

--- a/solution.py
+++ b/solution.py
@@ -172,7 +172,7 @@
             remote(gath.at[band], gath.at[band], BAND + d, BAND + d, {"dom": me, "band": (band + d) % n_band}),
             None, None,
         )
-        for d in range(1, n_band)
+        for d in sorted(range(1, n_band), key=lambda d: -min(d, n_band - d))
     ]
 
     cp_prev.wait()
@@ -315,7 +315,7 @@
     tot[...] = rho
     totb[...] = packed(rho)
     halo_in = []
-    for dx, dy, dz in OFFSETS:
+    for dx, dy, dz in sorted(OFFSETS, key=lambda o: (-abs(o[0]) - abs(o[1]), -abs(o[0]), -o[2])):
         there = slot_of(-dx, -dy, dz)
         cols = {0: pl.ds(0, YZ), -1: pl.ds(0, 256), 1: pl.ds(YZ - 256, 256)}[dy]
         cp = remote(
@@ -363,31 +363,30 @@
         last = jnp.where(lane < 64, pltpu.roll(v, 16 + M - FZ + LANES, 1), pltpu.roll(s, 80 + M - FZ + LANES, 1))
         zsend[x] = jnp.where(inner, first, last).astype(BF16)
 
-    loop(0, NX, pack_z, 2)
+    loop(0, NX, pack_z, 11)
     z_in = send(remote(zsend, zrecv, POT_Z, POT_Z, neighbour(0, 0, 1)), None, None)
 
     for x in range(BX):
         base[x : x + 1, :] = loc[x]
     base[...] = base[...] - jnp.exp(jnp.log((3.0 / math.pi) * tot[...]) * (1.0 / 3.0))
 
-    def stencil_of(x):
+    arrive(*orb_in)
+    for first in (0, 3):
+        group = slice(first, first + 3)
         for t in range(3):
             if t == 0:
-                here = [ylo[x], waves[x, :, 0:512]]
+                here = [ylo[group], waves[group, :, 0:512]]
             elif t == 1:
-                here = [waves[x, :, 256:896]]
+                here = [waves[group, :, 256:896]]
             else:
-                here = [waves[x, :, 640:1152], yhi[x]]
+                here = [waves[group, :, 640:1152], yhi[group]]
             cols = slice(384 * t, 384 * (t + 1))
-            lhs = jnp.concatenate([*here, zbuf[x, :, cols]], 1)
-            out = jnp.dot(lhs, w_ref[...], preferred_element_type=F32)
-            below = xlo[:, cols] if x == 0 else waves[x - 1, :, cols]
-            above = xhi[:, cols] if x == BX - 1 else waves[x + 1, :, cols]
-            stencil[x, :, cols] = out - 0.5 * (below.astype(F32) + above.astype(F32))
-
-    arrive(*orb_in)
-    for x in range(1, BX - 1):
-        stencil_of(x)
+            lhs = jnp.concatenate([*here, zbuf[group, :, cols]], 2).reshape(3 * nb, 1024)
+            out = jnp.dot(lhs, w_ref[...], preferred_element_type=F32).reshape(3, nb, 384)
+            for u in range(3):
+                x = first + u
+                sides = [waves[other, :, cols].astype(F32) for other in (x - 1, x + 1) if 0 <= other < BX]
+                stencil[x, :, cols] = out[u] - 0.5 * sum(sides[1:], sides[0])
 
     arrive(z_in)
     from_z = jnp.where(bk == 0, jnp.where((lane >= FZ) & (lane < FZ + M), 1, 0), jnp.where(lane >= LANES - M, 1, 0)) == 1
@@ -399,11 +398,11 @@
         va[x, span, :] = jnp.where(from_z, pltpu.roll(rim, shift_v, 1), va[x, span, :])
         sa[x, span, :] = jnp.where(from_z, pltpu.roll(rim, shift_s, 1), sa[x, span, :])
 
-    loop(0, NX, merge, 2)
+    loop(0, NX, merge, 11)
 
     arrive(*orb_x_in)
-    stencil_of(0)
-    stencil_of(BX - 1)
+    stencil[0] = stencil[0] - 0.5 * xlo[...].astype(F32)
+    stencil[BX - 1] = stencil[BX - 1] - 0.5 * xhi[...].astype(F32)
 
     arrive(*halo_in)
     for dst, dz in ((xo, 0), (xz, 1)):
@@ -424,7 +423,7 @@
             for q in range(8):
                 cbuf[g * 8 + q, :, base : base + BZ] = block[:, 112 + BZ * q : 112 + BZ * (q + 1)]
 
-    loop(0, 4, split_rho, 2)
+    loop(0, 4, split_rho, 4)
     source_row = iota((LANES, LANES), 0)
     fine_lane = iota((LANES, LANES), 1)
     fine_z = jnp.where(fine_lane >= LANES - M, fine_lane - LANES, fine_lane)
@@ -448,7 +447,7 @@
         f2[x, pl.ds(4, 28, stride=2), :] = mid + 0.25 * block[5:33]
         f2[x, pl.ds(5, 28, stride=2), :] = mid + 0.25 * block[7:35]
 
-    loop(0, 12, refine_y, 4)
+    loop(0, 12, refine_y, 12)
 
     def refine_x(x):
         mid = 0.75 * f2[x]
@@ -456,7 +455,7 @@
         sa[at, span, :] = sa[at, span, :] + mid + 0.25 * f2[x - 1]
         sa[at + 1, span, :] = sa[at + 1, span, :] + mid + 0.25 * f2[x + 1]
 
-    loop(1, 11, refine_x, 5)
+    loop(1, 11, refine_x, 10)
 
     yrow = iota((SPAN, LANES), 0)
     y_ok = ((yrow >= 8) | has_ylo) & ((yrow < 8 + FY) | has_yhi)
@@ -476,7 +475,7 @@
             factor = jnp.where(x < M, x_low, jnp.where(x >= M + FX, x_high, 1.0))
             new[x, span, :] = acc * (sixth * factor)
 
-        loop(1 + sweep, NX - 1 - sweep, update, (5, 6, 4, 7)[sweep])
+        loop(1 + sweep, NX - 1 - sweep, update, NX - 2 - 2 * sweep)
 
     for x in range(BX):
         at = 2 * x + M
@@ -507,6 +506,21 @@
     loop(0, FX, join, 6)
 
     finish()
+
+
+def apply_kernel(stencil, effective, waves, potential, applied_out, potential_out, applied, sem):
+    cp_pot = pltpu.make_async_copy(potential, potential_out, sem.at[BX])
+    cp_pot.start()
+    copies = []
+    for x in range(BX):
+        here = stencil[x] + effective[x : x + 1, :] * waves[x].astype(F32)
+        applied[x] = here.astype(BF16)
+        cp = pltpu.make_async_copy(applied.at[x], applied_out.at[x], sem.at[x])
+        cp.start()
+        copies.append(cp)
+    for cp in copies:
+        cp.wait()
+    cp_pot.wait()
 
 
 def solution(mesh):
@@ -583,7 +597,17 @@
             pltpu.with_memory_space_constraint(compensation.reshape(OWN, LANES), pltpu.HBM),
             pltpu.with_memory_space_constraint(local_potential.reshape(BX, 1, YZ), pltpu.HBM),
         )
-        applied = (stencil + effective[:, None] * held.astype(F32)).astype(BF16)
+        applied, potential = pl.pallas_call(
+            apply_kernel,
+            out_shape=(
+                jax.ShapeDtypeStruct((BX, nb, YZ), BF16),
+                jax.ShapeDtypeStruct((OWN, LANES), F32),
+            ),
+            in_specs=[vmem] * 4,
+            out_specs=(hbm, hbm),
+            scratch_shapes=[pltpu.VMEM((BX, nb, YZ), BF16), pltpu.SemaphoreType.DMA((BX + 1,))],
+            compiler_params=pltpu.CompilerParams(vmem_limit_bytes=8 * 1024 * 1024),
+        )(stencil, effective, held, potential)
         return applied.transpose(1, 0, 2)[:, None], potential.reshape(previous.shape)
 
     return jax.shard_map(

time: 27.1 us -> 23.4 us (0.86)
  Pallas kernels: 24.2 us -> 22.5 us
  other arithmetic: 1.48 us -> 0 us
  local copies, waits for them, and re-layouts: 0.68 us -> 0 us
    pallas_call x1, Pallas kernels: 24.2 us -> 21.3 us  [local(): pl.pallas_call(functools.partial(step_kernel, (nb, n_band, nx, ny)), out_...]
    broadcast_in_dim x1 -> x0, other arithmetic: 1.48 us -> none  [local(): applied.transpose(1, 0, 2)[:, None]]
    pallas_call x0 -> x1, Pallas kernels: none -> 1.19 us  [local(): pl.pallas_call(apply_kernel, out_shape=(jax.ShapeDtypeStruct((BX, nb, YZ)...]
    unnamed x1 -> x0, local copies, waits for them, and re-layouts: 0.68 us -> none
where the time goes in v4:
time: 23.4 us; the launch traced here: 23.1 us
  Pallas kernels  22.5 us (96%)
  between operations  0.64 us (3%)
    pallas_call x1, Pallas kernels, local(): pl.pallas_call(functools.partial(step_kernel, (nb, n_band, nx, ny)), out_...  21.3 us
    pallas_call x1, Pallas kernels, local(): pl.pallas_call(apply_kernel, out_shape=(jax.ShapeDtypeStruct((BX, nb, YZ)...  1.19 us

profile of v4, /device:TPU:1, one launch (start us, length us, event | category | flops | bytes accessed | tf_op | source)
XLA Modules:
  0.0 23.1 jit_solution(6482963010748366066)
XLA Ops:
  0.6 21.3 %shard_map.68 = (f32[6,96,1152]{2,1,0:T(8,128)S(1)}, f32[6,1152]{1,0:T(8,128)S(1)}, f32[432,128]{1,0:T(8,128)S(1)}, bf16[6,96,1152]{2,1,0:T(8,128)(2,1)S(1)}) custom-call(bf16[6,96,1152]{2,1,0:T(8,128)(2,1)} %bitcast.11, f32[1,96]{1,0:T(1,128)} %bitcast.15, f32[432,128]{1,0:T(8,128)} %bitcast.12, f32[432,128]{1,0:T(8,128)} %bitcast.13, f32[6,1,1152]{2,1,0:T(1,128)} %bitcast.14), custom_call_target="tpu_custom_call" | custom-call | tf_op jit(solution)/shard_map/pallas_call | solution.py:537
  21.9 1.2 %shard_map.69 = (bf16[6,96,1152]{2,1,0:T(8,128)(2,1)}, f32[432,128]{1,0:T(8,128)}) custom-call(f32[6,96,1152]{2,1,0:T(8,128)S(1)} %get-tuple-element.8.stencil, f32[6,1152]{1,0:T(8,128)S(1)} %get-tuple-element.9.effective, bf16[6,96,1152]{2,1,0:T(8,128)(2,1)S(1)} %get-tuple-element.10.waves, f32[432,128]{1,0:T(8,128)S(1)} %get-tuple-element.11.potential), custom_call_target="tpu_custom_call" | custom-call | tf_op jit(solution)/shard_map/pallas_call | solution.py:600

commit v5 on v4

--- a/solution.py
+++ b/solution.py
@@ -198,7 +198,7 @@
             at = EDGE + 36 * x
             rim_tmp[0, n, 4 * x : 4 * x + 4, :] = src[at : at + 4, :]
             rim_tmp[1, n, 4 * x : 4 * x + 4, :] = src[at + 32 : at + 36, :]
-    rim_out[...] = rim_tmp[...].astype(BF16)
+    rim_out[...] = rim_tmp[:, :, 0:48, :].astype(BF16)
     rim_copies = []
     for side, dy in ((0, -1), (1, 1)):
         for dx in (0, -1, 1):
@@ -335,13 +335,13 @@
     arrive(*rim_copies)
     lane22 = iota((NX, LANES), 1)
     for n, (_, dst, scale) in enumerate(fields):
-        flat = dst.reshape(NX * YROWS, LANES)
+        flat = dst.reshape((NX + 2) * YROWS, LANES)
         for side in range(2):
             rim_tmp[0, 0, 0:20, :] = rim_in[0, side, n].astype(F32)[28:48]
             rim_tmp[0, 0, 20:48, :] = rim_in[1, side, n].astype(F32)[0:28]
             rim_tmp[0, 1, 0:20, :] = rim_in[1, side, n].astype(F32)[28:48]
             rim_tmp[0, 1, 20:40, :] = rim_in[2, side, n].astype(F32)[0:20]
-            rim_all[side, n, 0:48, :] = rim_tmp[0, 0]
+            rim_all[side, n, 0:48, :] = rim_tmp[0, 0, 0:48, :]
             rim_all[side, n, 48:88, :] = rim_tmp[0, 1, 0:40, :]
             a = [scale * rim_all[side, n, pl.ds(r, NX, stride=4), :] for r in range(4)]
             if side == 0:
@@ -400,9 +400,6 @@
 
     loop(0, NX, merge, 11)
 
-    arrive(*orb_x_in)
-    stencil[0] = stencil[0] - 0.5 * xlo[...].astype(F32)
-    stencil[BX - 1] = stencil[BX - 1] - 0.5 * xhi[...].astype(F32)
 
     arrive(*halo_in)
     for dst, dz in ((xo, 0), (xz, 1)):
@@ -450,10 +447,10 @@
     loop(0, 12, refine_y, 12)
 
     def refine_x(x):
-        mid = 0.75 * f2[x]
+        mid = 0.75 * f2[x, 0:SPAN, :]
         at = 2 * x - 1
-        sa[at, span, :] = sa[at, span, :] + mid + 0.25 * f2[x - 1]
-        sa[at + 1, span, :] = sa[at + 1, span, :] + mid + 0.25 * f2[x + 1]
+        sa[at, span, :] = sa[at, span, :] + mid + 0.25 * f2[x - 1, 0:SPAN, :]
+        sa[at + 1, span, :] = sa[at + 1, span, :] + mid + 0.25 * f2[x + 1, 0:SPAN, :]
 
     loop(1, 11, refine_x, 10)
 
@@ -476,6 +473,10 @@
             new[x, span, :] = acc * (sixth * factor)
 
         loop(1 + sweep, NX - 1 - sweep, update, NX - 2 - 2 * sweep)
+
+    arrive(*orb_x_in)
+    stencil[0] = stencil[0] - 0.5 * xlo[...].astype(F32)
+    stencil[BX - 1] = stencil[BX - 1] - 0.5 * xhi[...].astype(F32)
 
     for x in range(BX):
         at = 2 * x + M
@@ -490,7 +491,7 @@
     wr = jnp.where((rel == 0) | (rel == 1), 0.375, 0.0)
     wr = jnp.where((rel == -1) | (rel == 2), 0.125, wr)
     wr = jnp.where(cell < BZ, wr, 0.0)
-    c3[...] = jnp.dot(c3[...], wr, precision=EXACT, preferred_element_type=F32)
+    c3[0 : BX * BY, :] = jnp.dot(c3[0 : BX * BY, :], wr, precision=EXACT, preferred_element_type=F32)
     for y in range(BY):
         tmp_m[0:BX, y * BZ : (y + 1) * BZ] = c3[pl.ds(y, BX, stride=BY), :][:, 0:BZ]
     eff_out[...] = tmp_m[0:BX, :] + base[0:BX, :]
@@ -509,7 +510,7 @@
 
 
 def apply_kernel(stencil, effective, waves, potential, applied_out, potential_out, applied, sem):
-    cp_pot = pltpu.make_async_copy(potential, potential_out, sem.at[BX])
+    cp_pot = pltpu.make_async_copy(potential.at[pl.ds(0, OWN)], potential_out, sem.at[BX])
     cp_pot.start()
     copies = []
     for x in range(BX):
@@ -539,7 +540,7 @@
             out_shape=(
                 jax.ShapeDtypeStruct((BX, nb, YZ), F32),
                 jax.ShapeDtypeStruct((BX, YZ), F32),
-                jax.ShapeDtypeStruct((OWN, LANES), F32),
+                jax.ShapeDtypeStruct((OWN + 16, LANES), F32),
                 jax.ShapeDtypeStruct((BX, nb, YZ), BF16),
             ),
             in_specs=[hbm] * 5,
@@ -561,12 +562,12 @@
                 pltpu.VMEM((2, EDGE, LANES), BF16),
                 pltpu.VMEM((BX, 1, YZ), F32),
             ]
-            + [pltpu.VMEM((NX, YROWS, LANES), F32)] * 3
+            + [pltpu.VMEM((NX + 2, YROWS, LANES), F32)] * 3
             + [
-                pltpu.VMEM((2, 2, 48, LANES), F32),
+                pltpu.VMEM((2, 2, 56, LANES), F32),
                 pltpu.VMEM((2, 2, 48, LANES), BF16),
                 pltpu.VMEM((3, 2, 2, 48, LANES), BF16),
-                pltpu.VMEM((2, 2, 88, LANES), F32),
+                pltpu.VMEM((2, 2, 96, LANES), F32),
                 pltpu.VMEM((NX, SPAN, LANES), BF16),
                 pltpu.VMEM((NX, SPAN, LANES), BF16),
                 pltpu.VMEM((8, YZ), F32),
@@ -577,10 +578,10 @@
                 pltpu.VMEM((16, 512 + YZ), F32),
                 pltpu.VMEM((16, 512 + YZ), F32),
                 pltpu.VMEM((32, 16, LANES), F32),
-                pltpu.VMEM((12 * 40, LANES), F32),
-                pltpu.VMEM((12, SPAN, LANES), F32),
+                pltpu.VMEM((16 * 40, LANES), F32),
+                pltpu.VMEM((12, SPAN + 8, LANES), F32),
                 pltpu.VMEM((BX, YROWS, LANES), F32),
-                pltpu.VMEM((BX * BY, LANES), F32),
+                pltpu.VMEM((8 * BY, LANES), F32),
                 pltpu.VMEM((8, YZ), F32),
                 pltpu.VMEM((8, YZ), F32),
                 pltpu.SemaphoreType.DMA((BX + 4,)),

time: 23.4 us -> 23.4 us (level)
  no operation moved by 1% of the time
where the time goes in v5:
time: 23.4 us; the launch traced here: 23.3 us
  Pallas kernels  22.7 us (97%)
  between operations  0.64 us (3%)
    pallas_call x1, Pallas kernels, local(): pl.pallas_call(functools.partial(step_kernel, (nb, n_band, nx, ny)), out_...  21.5 us
    pallas_call x1, Pallas kernels, local(): pl.pallas_call(apply_kernel, out_shape=(jax.ShapeDtypeStruct((BX, nb, YZ)...  1.19 us

profile of v5, /device:TPU:1, one launch (start us, length us, event | category | flops | bytes accessed | tf_op | source)
XLA Modules:
  0.0 23.3 jit_solution(6321956504350948606)
XLA Ops:
  0.6 21.5 %shard_map.68 = (f32[6,96,1152]{2,1,0:T(8,128)S(1)}, f32[6,1152]{1,0:T(8,128)S(1)}, f32[448,128]{1,0:T(8,128)S(1)}, bf16[6,96,1152]{2,1,0:T(8,128)(2,1)S(1)}) custom-call(bf16[6,96,1152]{2,1,0:T(8,128)(2,1)} %bitcast.11, f32[1,96]{1,0:T(1,128)} %bitcast.15, f32[432,128]{1,0:T(8,128)} %bitcast.12, f32[432,128]{1,0:T(8,128)} %bitcast.13, f32[6,1,1152]{2,1,0:T(1,128)} %bitcast.14), custom_call_target="tpu_custom_call" | custom-call | tf_op jit(solution)/shard_map/pallas_call | solution.py:538
  22.1 1.2 %shard_map.69 = (bf16[6,96,1152]{2,1,0:T(8,128)(2,1)}, f32[432,128]{1,0:T(8,128)}) custom-call(f32[6,96,1152]{2,1,0:T(8,128)S(1)} %get-tuple-element.8.stencil, f32[6,1152]{1,0:T(8,128)S(1)} %get-tuple-element.9.effective, bf16[6,96,1152]{2,1,0:T(8,128)(2,1)S(1)} %get-tuple-element.10.waves, f32[448,128]{1,0:T(8,128)S(1)} %get-tuple-element.11.potential), custom_call_target="tpu_custom_call" | custom-call | tf_op jit(solution)/shard_map/pallas_call | solution.py:601

commit v6 on v5

--- a/solution.py
+++ b/solution.py
@@ -49,6 +49,10 @@
         return carry
 
     assert (high - low) % together == 0
+    if together == high - low:
+        for i in range(low, high):
+            body(i)
+        return
     lax.fori_loop(0, (high - low) // together, some, 0)
 
 
@@ -469,8 +473,12 @@
             acc = old[x - 1, span, :] + old[x + 1, span, :] + sa[x, span, :]
             acc = acc + (old[x, Y0 - 9 : Y0 - 9 + SPAN, :] + old[x, Y0 - 7 : Y0 - 7 + SPAN, :])
             acc = acc + pltpu.roll(mid, 1, 1) + pltpu.roll(mid, LANES - 1, 1)
-            factor = jnp.where(x < M, x_low, jnp.where(x >= M + FX, x_high, 1.0))
-            new[x, span, :] = acc * (sixth * factor)
+            factor = sixth
+            if x < M:
+                factor = sixth * x_low
+            elif x >= M + FX:
+                factor = sixth * x_high
+            new[x, span, :] = acc * factor
 
         loop(1 + sweep, NX - 1 - sweep, update, NX - 2 - 2 * sweep)
 

time: 23.4 us -> 23.4 us (level)
  no operation moved by 1% of the time
where the time goes in v6:
time: 23.4 us; the launch traced here: 23.3 us
  Pallas kernels  22.7 us (97%)
  between operations  0.64 us (3%)
    pallas_call x1, Pallas kernels, local(): pl.pallas_call(functools.partial(step_kernel, (nb, n_band, nx, ny)), out_...  21.5 us
    pallas_call x1, Pallas kernels, local(): pl.pallas_call(apply_kernel, out_shape=(jax.ShapeDtypeStruct((BX, nb, YZ)...  1.19 us

profile of v6, /device:TPU:1, one launch (start us, length us, event | category | flops | bytes accessed | tf_op | source)
XLA Modules:
  0.0 23.3 jit_solution(6321956504350948606)
XLA Ops:
  0.6 21.5 %shard_map.68 = (f32[6,96,1152]{2,1,0:T(8,128)S(1)}, f32[6,1152]{1,0:T(8,128)S(1)}, f32[448,128]{1,0:T(8,128)S(1)}, bf16[6,96,1152]{2,1,0:T(8,128)(2,1)S(1)}) custom-call(bf16[6,96,1152]{2,1,0:T(8,128)(2,1)} %bitcast.11, f32[1,96]{1,0:T(1,128)} %bitcast.15, f32[432,128]{1,0:T(8,128)} %bitcast.12, f32[432,128]{1,0:T(8,128)} %bitcast.13, f32[6,1,1152]{2,1,0:T(1,128)} %bitcast.14), custom_call_target="tpu_custom_call" | custom-call | tf_op jit(solution)/shard_map/pallas_call | solution.py:546
  22.1 1.2 %shard_map.69 = (bf16[6,96,1152]{2,1,0:T(8,128)(2,1)}, f32[432,128]{1,0:T(8,128)}) custom-call(f32[6,96,1152]{2,1,0:T(8,128)S(1)} %get-tuple-element.8.stencil, f32[6,1152]{1,0:T(8,128)S(1)} %get-tuple-element.9.effective, bf16[6,96,1152]{2,1,0:T(8,128)(2,1)S(1)} %get-tuple-element.10.waves, f32[448,128]{1,0:T(8,128)S(1)} %get-tuple-element.11.potential), custom_call_target="tpu_custom_call" | custom-call | tf_op jit(solution)/shard_map/pallas_call | solution.py:609
